TPU v7x, 128 devices: a whole 4x4x4 slice. The times are simulated.
128 devices in a mesh: fsdp: 16 (over x, z), tp: 8 (over y, core).
Axes of the slice: x: 4, y: 4, z: 4, core: 2. Of those that a mesh axis runs over, the one named last changes fastest.
Arguments:
- weights: float32 [16384, 16384], P('fsdp', 'tp'), may hold values from -6 to 6
- owner: int32 [128], replicated, may hold values from 0 to 15, as said below
Outputs:
- rolled: bfloat16 [32768, 16384], P('fsdp', 'tp')
- rolled_scales: bfloat16 [256, 16384], P('fsdp', 'tp')
Inputs may be any that keep to these rules, and one draw needn't show every extreme that they name: Trainer shard a holds blocks a * 8 to a * 8 + 7, as 8 runs of 1 block with one owner each and a different owner for each run; one rollout rank owns exactly 16 blocks.
All inputs are finite; a program needn't handle non-finite values.
Results may differ from a plain program's by a relative error of at most 0.0085.
Values may be sent and summed in bfloat16 or wider, within the bound.
No kernel may reach another device: no remote copies, remote signals or barrier semaphores. Data moves between devices by JAX's collectives and lax.ppermute only.
A program may use at most 320 MiB of HBM per device.

v0:
```python
import math

import jax
import jax.numpy as jnp
from jax import lax
from jax.sharding import PartitionSpec as P

K = 16384
BLOCK = 128
TILE = 128


def swapped(value, axis, distance):
    mask = 2**distance
    pairs = [(source, source ^ mask) for source in range(lax.axis_size(axis))]
    return lax.ppermute(value, axis, pairs)


def signs_table(length):
    indices = jnp.arange(length, dtype=jnp.int32)
    common_bits = indices[:, None] & indices[None, :]
    parity = jnp.zeros((length, length), jnp.int32)
    for bit_index in range(length.bit_length() - 1):
        parity = parity ^ common_bits >> bit_index & 1
    return (1 - 2 * parity).astype(jnp.float32)


def per_device(weights, owner):
    fsdp_size = lax.axis_size("fsdp")
    tp_size = lax.axis_size("tp")
    position = lax.axis_index("fsdp")
    row_count, col_count = weights.shape
    highest = lax.Precision.HIGHEST
    rotated = jnp.dot(signs_table(row_count), weights, precision=highest)
    for bit_index in range(fsdp_size.bit_length() - 1):
        partner = swapped(rotated, "fsdp", bit_index)
        lower_half = position >> bit_index & 1 == 0
        rotated = jnp.where(lower_half, rotated + partner, partner - rotated)
    rotated = rotated * (1.0 / math.sqrt(K))
    block_count = row_count // BLOCK
    grouped = rotated.reshape(block_count, BLOCK, col_count)
    largest = jnp.max(jnp.abs(grouped), axis=1)
    scales = (largest + 1e-06).astype(jnp.bfloat16)
    quantized = (grouped / scales.astype(jnp.float32)[:, None, :]).astype(jnp.bfloat16)
    pair_slots = max(1, 2 * block_count // fsdp_size)
    my_owners = lax.dynamic_slice_in_dim(owner, position * block_count, block_count)
    locals_index = jnp.arange(block_count, dtype=jnp.int32)
    earlier = (my_owners[:, None] == my_owners[None, :]) & (
        locals_index[None, :] < locals_index[:, None]
    )
    target = my_owners * pair_slots + jnp.sum(earlier.astype(jnp.int32), axis=1)
    slot_index = jnp.arange(fsdp_size * pair_slots, dtype=jnp.int32)
    chooser = (slot_index[:, None] == target[None, :]).astype(jnp.bfloat16)
    outgoing = jnp.dot(
        chooser,
        quantized.reshape(block_count, BLOCK * col_count),
        preferred_element_type=jnp.float32,
    ).astype(jnp.bfloat16)
    outgoing_scales = jnp.dot(chooser, scales, preferred_element_type=jnp.float32).astype(
        jnp.bfloat16
    )
    col_tiles = col_count // (TILE * tp_size)
    outgoing = outgoing.reshape(fsdp_size, pair_slots * BLOCK, col_tiles, tp_size, TILE)
    outgoing_scales = outgoing_scales.reshape(fsdp_size, pair_slots, col_tiles, tp_size, TILE)
    incoming, incoming_scales = (
        lax.all_to_all(
            lax.all_to_all(outgoing, "fsdp", split_axis=0, concat_axis=0, tiled=True),
            "tp",
            split_axis=3,
            concat_axis=2,
            tiled=True,
        ),
        lax.all_to_all(
            lax.all_to_all(outgoing_scales, "fsdp", split_axis=0, concat_axis=0, tiled=True),
            "tp",
            split_axis=3,
            concat_axis=2,
            tiled=True,
        ),
    )
    rolled = incoming.reshape(fsdp_size * pair_slots * BLOCK, col_count)
    rolled_scales = incoming_scales.reshape(fsdp_size * pair_slots, col_count)
    return (rolled, rolled_scales)


def solution(mesh):
    return jax.shard_map(
        per_device,
        mesh=mesh,
        in_specs=(P("fsdp", "tp"), P()),
        out_specs=(P("fsdp", "tp"), P("fsdp", "tp")),
        check_vma=False,
    )
```

profile of v0, /device:TPU:6, one launch (start us, length us, event | category | flops | bytes accessed | tf_op | source)
XLA Modules:
  0.0 1119.0 jit_solution(9288429810888296840)
XLA Ops:
  0.6 47.3 %fusion.1 = f32[1024,2048]{1,0:T(8,128)} fusion(f32[1024,2048]{1,0:T(8,128)} %param.2), kind=kOutput, calls=%fused_computation.8 | convolution fusion | flops 25804406784 | bytes 16777216 | tf_op jit(solution)/shard_map/dot_general | solution.py:34
  49.9 180.8 %collective-permute-done = f32[1024,2048]{1,0:T(8,128)} collective-permute-done((f32[1024,2048]{1,0:T(8,128)}, f32[1024,2048]{1,0:T(8,128)}, u32[]{:S(2)}, u32[]{:S(2)}) %collective-permute-start) | collective-permute-done | bytes 8388640 | tf_op jit(solution)/shard_map/ppermute | solution.py:16
  230.6 12.1 %subtract_select_fusion.2 = f32[1024,2048]{1,0:T(8,128)} fusion(f32[1024,2048]{1,0:T(8,128)} %collective-permute-done, f32[1024,2048]{1,0:T(8,128)} %fusion.1, pred[]{:T(512)S(6)} %eq.47), kind=kLoop, calls=%fused_computation.6 | loop fusion | flops 6291456 | bytes 25165824 | tf_op jit(solution)/shard_map/jit(_where)/select_n | solution.py:38
  242.7 3.7 collective-permute-start.1
  246.4 179.9 %collective-permute-done.1 = f32[1024,2048]{1,0:T(8,128)} collective-permute-done((f32[1024,2048]{1,0:T(8,128)}, f32[1024,2048]{1,0:T(8,128)}, u32[]{:S(2)}, u32[]{:S(2)}) %collective-permute-start.1) | collective-permute-done | bytes 8388640 | tf_op jit(solution)/shard_map/ppermute | solution.py:16
  426.3 12.1 %subtract_select_fusion.1 = f32[1024,2048]{1,0:T(8,128)} fusion(f32[1024,2048]{1,0:T(8,128)} %collective-permute-done.1, f32[1024,2048]{1,0:T(8,128)} %subtract_select_fusion.2, pred[]{:T(512)S(6)} %eq.46), kind=kLoop, calls=%fused_computation.5 | loop fusion | flops 6291456 | bytes 25165824 | tf_op jit(solution)/shard_map/jit(_where)/select_n | solution.py:38
  439.2 180.3 %collective-permute-done.2 = f32[1024,2048]{1,0:T(8,128)} collective-permute-done((f32[1024,2048]{1,0:T(8,128)}, f32[1024,2048]{1,0:T(8,128)}, u32[]{:S(2)}, u32[]{:S(2)}) %collective-permute-start.2) | collective-permute-done | bytes 8388640 | tf_op jit(solution)/shard_map/ppermute | solution.py:16
  619.4 12.1 %subtract_select_fusion = f32[1024,2048]{1,0:T(8,128)} fusion(f32[1024,2048]{1,0:T(8,128)} %collective-permute-done.2, f32[1024,2048]{1,0:T(8,128)} %subtract_select_fusion.1, pred[]{:T(512)S(6)} %eq.45), kind=kLoop, calls=%fused_computation.4 | loop fusion | flops 6291456 | bytes 25165824 | tf_op jit(solution)/shard_map/jit(_where)/select_n | solution.py:38
  633.3 180.0 %collective-permute-done.3 = f32[1024,2048]{1,0:T(8,128)} collective-permute-done((f32[1024,2048]{1,0:T(8,128)}, f32[1024,2048]{1,0:T(8,128)}, u32[]{:S(2)}, u32[]{:S(2)}) %collective-permute-start.3) | collective-permute-done | bytes 8388640 | tf_op jit(solution)/shard_map/ppermute | solution.py:16
  813.2 10.1 bitcast_reduce_fusion
  823.3 8.1 reshape.33
  832.2 7.1 all-to-all-start.2
  839.3 4.4 div.11
  843.8 11.3 %fusion = bf16[2,8,2048,128]{3,1,2,0:T(8,128)(2,1)} fusion(f32[8,262144]{1,0:T(8,128)} %reshape.33, f32[8,262144]{1,0:T(8,128)} %bitcast.26, s32[8]{0:T(128)S(1)} %dynamic-slice_add_fusion), kind=kOutput, calls=%fused_computation.7 | convolution fusion | flops 75497600 | bytes 25165856 | tf_op jit(solution)/shard_map/dot_general | solution.py:54
  855.1 8.3 copy.31
  863.3 13.0 %copy.22 = bf16[16,128,2,8,128]{4,2,1,3,0:T(2,128)(2,1)} copy(bf16[16,128,2,8,128]{4,3,2,1,0:T(8,128)(2,1)} %bitcast.25) | data formatting | bytes 16777216 | tf_op jit(solution)/shard_map/reshape | solution.py:63
  876.4 7.2 all-to-all-start
  884.3 100.1 %all-to-all-done = bf16[16,128,2,8,128]{4,2,1,3,0:T(2,128)(2,1)} async-done(((bf16[16,128,2,8,128]{4,2,1,3,0:T(2,128)(2,1)}), bf16[16,128,2,8,128]{4,2,1,3,0:T(2,128)(2,1)}, u32[]{:S(2)}, u32[]{:S(2)}) %all-to-all-start) | async-done | bytes 8388640 | tf_op jit(solution)/shard_map/all_to_all | solution.py:67
  984.4 4.4 all-to-all-start.3
  988.8 8.2 copy.23
  997.0 5.0 all-to-all-start.1
  1002.6 93.9 %all-to-all-done.1 = bf16[16,128,2,8,128]{4,2,1,0,3:T(2,128)(2,1)} async-done(((bf16[16,128,2,8,128]{4,2,1,0,3:T(2,128)(2,1)}), bf16[16,128,2,8,128]{4,2,1,0,3:T(2,128)(2,1)}, u32[]{:S(2)}, u32[]{:S(2)}) %all-to-all-start.1) | async-done | bytes 8388640 | tf_op jit(solution)/shard_map/all_to_all | solution.py:66
  1096.5 8.1 copy.29
  1104.6 14.4 %reshape.38 = bf16[2048,2048]{1,0:T(8,128)(2,1)} reshape(bf16[16,128,8,2,1,128]{5,3,2,1,0,4:T(2,128)(2,1)} %copy.29) | data formatting | bytes 16777216
  (16 shorter events, 6.7 us)
Async XLA Ops:
  47.9 182.7 %collective-permute-start = (f32[1024,2048]{1,0:T(8,128)}, f32[1024,2048]{1,0:T(8,128)}, u32[]{:S(2)}, u32[]{:S(2)}) collective-permute-start(f32[1024,2048]{1,0:T(8,128)} %fusion.1), channel_id=1, source_target_pairs={{0,8},{8,0},{16,24},{24,16},{32,40},{40,32},{48,56},{56,48},{64,72... | collective-permute-start | bytes 25165832 | tf_op jit(solution)/shard_map/ppermute | solution.py:16
  242.7 183.6 %collective-permute-start.1 = (f32[1024,2048]{1,0:T(8,128)}, f32[1024,2048]{1,0:T(8,128)}, u32[]{:S(2)}, u32[]{:S(2)}) collective-permute-start(f32[1024,2048]{1,0:T(8,128)} %subtract_select_fusion.2), channel_id=1, source_target_pairs={{0,16},{8,24},{16,0},{24,8},{32,48},{40,56},{48,32},{56,40},{64,80... | collective-permute-start | bytes 25165832 | tf_op jit(solution)/shard_map/ppermute | solution.py:16
  438.4 181.1 %collective-permute-start.2 = (f32[1024,2048]{1,0:T(8,128)}, f32[1024,2048]{1,0:T(8,128)}, u32[]{:S(2)}, u32[]{:S(2)}) collective-permute-start(f32[1024,2048]{1,0:T(8,128)} %subtract_select_fusion.1), channel_id=1, source_target_pairs={{0,32},{8,40},{16,48},{24,56},{32,0},{40,8},{48,16},{56,24},{64,96... | collective-permute-start | bytes 25165832 | tf_op jit(solution)/shard_map/ppermute | solution.py:16
  439.2 193.7 %copy-start = (s32[128]{0:T(128)S(1)}, s32[128]{0:T(128)}, u32[]{:S(2)}) copy-start(s32[128]{0:T(128)} %param.3) | copy-start | bytes 1540
  631.5 181.7 %collective-permute-start.3 = (f32[1024,2048]{1,0:T(8,128)}, f32[1024,2048]{1,0:T(8,128)}, u32[]{:S(2)}, u32[]{:S(2)}) collective-permute-start(f32[1024,2048]{1,0:T(8,128)} %subtract_select_fusion), channel_id=1, source_target_pairs={{0,64},{8,72},{16,80},{24,88},{32,96},{40,104},{48,112},{56,120},{... | collective-permute-start | bytes 25165832 | tf_op jit(solution)/shard_map/ppermute | solution.py:16
  832.2 44.1 %all-to-all-start.2 = ((bf16[16,1,2,8,128]{4,3,2,1,0:T(8,128)(2,1)}), bf16[16,1,2,8,128]{4,3,2,1,0:T(8,128)(2,1)S(1)}, u32[]{:S(2)}, u32[]{:S(2)}) async-start(bf16[16,1,2,8,128]{4,3,2,1,0:T(8,128)(2,1)} %bitcast.4), calls=%async_computation.2 | async-start | bytes 131072 | tf_op jit(solution)/shard_map/all_to_all | solution.py:74
  876.4 108.0 %all-to-all-start = ((bf16[16,128,2,8,128]{4,2,1,3,0:T(2,128)(2,1)}), bf16[16,128,2,8,128]{4,2,1,3,0:T(2,128)(2,1)}, u32[]{:S(2)}, u32[]{:S(2)}) async-start(bf16[16,128,2,8,128]{4,2,1,3,0:T(2,128)(2,1)} %copy.22), calls=%async_computation | async-start | bytes 16777216 | tf_op jit(solution)/shard_map/all_to_all | solution.py:67
  984.4 12.6 %all-to-all-start.3 = ((bf16[16,1,2,8,128]{4,2,0,1,3:T(2,128)(2,1)}), bf16[16,1,2,8,128]{4,2,0,1,3:T(2,128)(2,1)S(1)}, u32[]{:S(2)}, u32[]{:S(2)}) async-start(bf16[16,1,2,8,128]{4,2,0,1,3:T(2,128)(2,1)} %copy.26), calls=%async_computation.3 | async-start | bytes 131072 | tf_op jit(solution)/shard_map/all_to_all | solution.py:73
  997.0 99.6 %all-to-all-start.1 = ((bf16[16,128,2,8,128]{4,2,1,0,3:T(2,128)(2,1)}), bf16[16,128,2,8,128]{4,2,1,0,3:T(2,128)(2,1)}, u32[]{:S(2)}, u32[]{:S(2)}) async-start(bf16[16,128,2,8,128]{4,2,1,0,3:T(2,128)(2,1)} %copy.23), calls=%async_computation.1 | async-start | bytes 16777216 | tf_op jit(solution)/shard_map/all_to_all | solution.py:66
where the time goes:
time: 1120 us
  waiting for transfers between devices  915 us (82%)
  local copies, waits for them, and re-layouts  66.6 us (6%)
  matrix products  58.8 us (5%)
  other arithmetic  46.6 us (4%)
  starting transfers between devices  31.6 us (3%)
    ppermute x4, waiting for transfers between devices, swapped(): return lax.ppermute(value, axis, pairs)  721 us
    all_to_all x1, waiting for transfers between devices, per_device(): lax.all_to_all(outgoing, 'fsdp', split_axis=0, concat_axis=0, tiled=True)  100 us
    all_to_all x1, waiting for transfers between devices, per_device(): lax.all_to_all(lax.all_to_all(outgoing, 'fsdp', split_axis=0, concat_axis...  93.9 us
    dot_general x1, matrix products, per_device(): rotated = jnp.dot(signs_table(row_count), weights, precision=highest)  47.3 us
    select_n x3, other arithmetic, per_device(): rotated = jnp.where(lower_half, rotated + partner, partner - rotated)  36.2 us
    unnamed x6, local copies, waits for them, and re-layouts  31.4 us
  transfers between devices with their start and end apart: 8, of which 6 were waited for; matrix products, arithmetic and copies ran while one was open for 4% of the time, Pallas kernels for 0%

commit v1 on v0

v1 whole, which is shorter than its diff:
```python
import functools

import jax
import jax.numpy as jnp
from jax import lax
from jax.experimental import pallas as pl
from jax.experimental.pallas import tpu as pltpu
from jax.sharding import PartitionSpec as P

BLOCK = 128
LANES = 128
GROUP = 16
EIGHT = 8
SHARDS = 16
F32 = jnp.float32
BF16 = jnp.bfloat16


def butterflies(values):
    values = list(values)
    span = 1
    while span < len(values):
        for base in range(0, len(values), 2 * span):
            for k in range(base, base + span):
                low, high = values[k], values[k + span]
                values[k], values[k + span] = low + high, low - high
        span *= 2
    return values


def swap_groups(arrays):
    arrays = list(arrays)
    group = lax.broadcasted_iota(jnp.int32, arrays[0].shape, 1) // GROUP
    for bit in (1, 2, 4):
        high_group = (group & bit) != 0
        shift = bit * GROUP
        for u in range(EIGHT):
            if u & bit:
                continue
            low, high = arrays[u], arrays[u | bit]
            arrays[u] = jnp.where(high_group, pltpu.roll(high, shift, 1), low)
            arrays[u | bit] = jnp.where(
                high_group, high, pltpu.roll(low, LANES - shift, 1)
            )
    return arrays


def swap_row_groups(value):
    row = lax.broadcasted_iota(jnp.int32, value.shape, 0)
    group = lax.broadcasted_iota(jnp.int32, value.shape, 1) // GROUP
    for bit in (1, 2, 4):
        row_bit = (row & bit) != 0
        group_bit = (group & bit) != 0
        shift = bit * GROUP
        up = pltpu.roll(pltpu.roll(value, EIGHT - bit, 0), shift, 1)
        down = pltpu.roll(pltpu.roll(value, bit, 0), LANES - shift, 1)
        value = jnp.where(row_bit == group_bit, value, jnp.where(row_bit, down, up))
    return value


def signs(size):
    both = lax.broadcasted_iota(jnp.int32, (size, size), 0) & lax.broadcasted_iota(
        jnp.int32, (size, size), 1
    )
    shift = size.bit_length() // 2
    while shift:
        both = both ^ (both >> shift)
        shift //= 2
    return (1 - 2 * (both & 1)).astype(F32).astype(BF16)


def local_kernel(w_ref, out_ref, sign_ref):
    @pl.when(pl.program_id(0) == 0)
    def _():
        sign_ref[...] = signs(256)

    rows = [
        jnp.dot(
            sign_ref[...],
            w_ref[pl.ds(256 * q, 256), :].astype(BF16),
            preferred_element_type=F32,
        )
        for q in range(4)
    ]
    rows = butterflies(rows)
    for tile in range(2):
        parts = [
            rows[j // 2][(j % 2) * BLOCK : (j % 2 + 1) * BLOCK, tile * LANES : (tile + 1) * LANES]
            * (1.0 / 32.0)
            for j in range(EIGHT)
        ]
        for g, part in enumerate(swap_groups(parts)):
            out_ref[0, g, tile] = part.astype(BF16)


def local_rotation(weights):
    rows, cols = weights.shape
    steps = cols // (2 * LANES)
    per_half = steps // 2
    return pl.pallas_call(
        local_kernel,
        grid=(steps,),
        in_specs=[pl.BlockSpec((rows, 2 * LANES), lambda s: (0, s))],
        out_specs=pl.BlockSpec(
            (1, EIGHT, 2, BLOCK, LANES),
            lambda s: (s // per_half, 0, s % per_half, 0, 0),
        ),
        out_shape=jax.ShapeDtypeStruct((2, EIGHT, EIGHT, BLOCK, LANES), BF16),
        scratch_shapes=[pltpu.VMEM((256, 256), BF16)],
        name="local_rotation",
    )(weights)


def quantize_kernel(owner_ref, in_ref, out_ref, held, scales, slots, slot_scales, sems):
    step = pl.program_id(0)

    @pl.when(step < EIGHT)
    def _():
        t = step
        for chunk in range(1):
            pass
        rotated = butterflies([in_ref[a, 0].astype(F32) for a in range(SHARDS)])
        for a in range(SHARDS):
            value = rotated[a] * 0.25
            largest = jnp.max(jnp.abs(value), axis=0, keepdims=True)
            scale = (largest + 1e-06).astype(BF16).astype(F32)
            scales[a, pl.ds(t, 1), :] = scale
            held[a, t] = (value * (1.0 / scale)).astype(BF16)

    @pl.when(step == 0)
    def _():
        slot_scales[...] = jnp.zeros_like(slot_scales)

    def send(a, buffer):
        return pltpu.make_async_copy(
            slots.at[buffer],
            out_ref.at[:, pl.ds(pl.multiple_of(a * BLOCK, BLOCK), BLOCK), :],
            sems.at[buffer],
        )

    @pl.when(step >= EIGHT)
    def _():
        a = step - EIGHT
        buffer = lax.rem(a, 2)

        @pl.when(a >= 2)
        def _():
            send(a - 2, buffer).wait()

        slots[buffer] = jnp.zeros(slots.shape[1:], BF16)
        blocks = swap_groups([held[a, t].astype(F32) for t in range(EIGHT)])
        block_scales = swap_row_groups(scales[a])
        for j in range(EIGHT):
            rank = owner_ref[a * EIGHT + j]
            slots[buffer, rank] = blocks[j].astype(BF16)
            slot_scales[rank, pl.ds(a, 1), :] = block_scales[j : j + 1]
        send(a, buffer).start()

    @pl.when(step == EIGHT + SHARDS - 1)
    def _():
        send(SHARDS - 2, 0).wait()
        send(SHARDS - 1, 1).wait()
        slots[0, :, pl.ds(0, SHARDS), :] = slot_scales[...].astype(BF16)
        last = pltpu.make_async_copy(
            slots.at[0, :, pl.ds(0, SHARDS), :],
            out_ref.at[:, pl.ds(SHARDS * BLOCK, SHARDS), :],
            sems.at[0],
        )
        last.start()
        last.wait()


def quantize_blocks(owner, received):
    out_rows = SHARDS * BLOCK + SHARDS
    return pl.pallas_call(
        quantize_kernel,
        grid_spec=pltpu.PrefetchScalarGridSpec(
            num_scalar_prefetch=1,
            grid=(EIGHT + SHARDS,),
            in_specs=[
                pl.BlockSpec(
                    (SHARDS, 1, BLOCK, LANES),
                    lambda s, _: (0, jnp.minimum(s, EIGHT - 1), 0, 0),
                )
            ],
            out_specs=pl.BlockSpec(memory_space=pl.ANY),
            scratch_shapes=[
                pltpu.VMEM((SHARDS, EIGHT, BLOCK, LANES), BF16),
                pltpu.VMEM((SHARDS, EIGHT, LANES), F32),
                pltpu.VMEM((2, SHARDS, BLOCK, LANES), BF16),
                pltpu.VMEM((SHARDS, SHARDS, LANES), F32),
                pltpu.SemaphoreType.DMA((2,)),
            ],
        ),
        out_shape=jax.ShapeDtypeStruct((SHARDS, out_rows, LANES), BF16),
        name="quantize_blocks",
    )(owner, received)


def place_kernel(in_ref, scale_in_ref, out_ref, scale_out_ref):
    for half in range(2):
        tiles = swap_groups([in_ref[half * EIGHT + g].astype(F32) for g in range(EIGHT)])
        for t in range(EIGHT):
            start = (2 * t + half) * LANES
            out_ref[:, start : start + LANES] = tiles[t].astype(BF16)

    @pl.when(pl.program_id(0) == 0)
    def _():
        for half in range(2):
            tiles = swap_groups(
                [scale_in_ref[half * EIGHT + g].astype(F32) for g in range(EIGHT)]
            )
            for t in range(EIGHT):
                start = (2 * t + half) * LANES
                scale_out_ref[:, start : start + LANES] = tiles[t].astype(BF16)


def place_columns(incoming):
    cols = SHARDS * LANES
    return pl.pallas_call(
        place_kernel,
        grid=(SHARDS,),
        in_specs=[
            pl.BlockSpec((SHARDS, BLOCK, LANES), lambda s: (0, s, 0)),
            pl.BlockSpec((SHARDS, SHARDS, LANES), lambda s: (0, BLOCK, 0)),
        ],
        out_specs=[
            pl.BlockSpec((BLOCK, cols), lambda s: (s, 0)),
            pl.BlockSpec((SHARDS, cols), lambda s: (0, 0)),
        ],
        out_shape=[
            jax.ShapeDtypeStruct((SHARDS * BLOCK, cols), BF16),
            jax.ShapeDtypeStruct((SHARDS, cols), BF16),
        ],
        name="place_columns",
    )(incoming, incoming)


def per_device(weights, owner):
    outgoing = local_rotation(weights).reshape(SHARDS * EIGHT, BLOCK, LANES)
    received = lax.all_to_all(outgoing, ("fsdp", "tp"), 0, 0, tiled=True)
    received = received.reshape(SHARDS, EIGHT, BLOCK, LANES)
    slotted = quantize_blocks(owner, received)
    incoming = lax.all_to_all(slotted, "fsdp", 0, 0, tiled=True)
    return tuple(place_columns(incoming))


def solution(mesh):
    return jax.shard_map(
        per_device,
        mesh=mesh,
        in_specs=(P("fsdp", "tp"), P()),
        out_specs=(P("fsdp", "tp"), P("fsdp", "tp")),
        check_vma=False,
    )
```

time: 1120 us -> 213 us (0.19)
  waiting for transfers between devices: 915 us -> 0 us
  blocking collectives: 0 us -> 163 us
  local copies, waits for them, and re-layouts: 66.6 us -> 0 us
  matrix products: 58.8 us -> 0 us
  other arithmetic: 46.6 us -> 0 us
  Pallas kernels: 0 us -> 45.9 us
  starting transfers between devices: 31.6 us -> 0 us
    ppermute x4 -> x0, waiting for transfers between devices: 721 us -> none  [swapped(): return lax.ppermute(value, axis, pairs)]
    all_to_all x4 -> x0, waiting for transfers between devices: 194 us -> none  [the longest x1 100 us: per_device(): lax.all_to_all(outgoing, 'fsdp', split_axis=0, concat_axis=0, tiled=True)]
    all_to_all x0 -> x2, blocking collectives: none -> 163 us  [the longest x1 101 us: per_device(): incoming = lax.all_to_all(slotted, 'fsdp', 0, 0, tiled=True)]
    dot_general x3 -> x0, matrix products: 58.8 us -> none  [the longest x1 47.3 us: per_device(): rotated = jnp.dot(signs_table(row_count), weights, precision=highest)]
    pallas_call x0 -> x3, Pallas kernels: none -> 45.9 us  [the longest x1 18.6 us: quantize_blocks(): pl.pallas_call(quantize_kernel, grid_spec=pltpu.PrefetchScalarGridSpec(nu...]
    select_n x3 -> x0, other arithmetic: 36.2 us -> none  [per_device(): rotated = jnp.where(lower_half, rotated + partner, partner - rotated)]
    unnamed x6 -> x0, local copies, waits for them, and re-layouts: 31.4 us -> none
    all_to_all x4 -> x0, starting transfers between devices: 23.7 us -> none  [the longest x1 7.24 us: per_device(): lax.all_to_all(outgoing, 'fsdp', split_axis=0, concat_axis=0, tiled=True)]
  transfers between devices with their start and end apart: 8 -> 0, of which waited for: 6 -> 0; matrix products, arithmetic and copies ran while one was open for 4% -> 0% of each run, Pallas kernels for 0% -> 0%
where the time goes in v1:
time: 213 us; the launch traced here: 210 us
  blocking collectives  163 us (77%)
  Pallas kernels  45.9 us (22%)
    all_to_all x1, blocking collectives, per_device(): incoming = lax.all_to_all(slotted, 'fsdp', 0, 0, tiled=True)  101 us
    all_to_all x1, blocking collectives, per_device(): received = lax.all_to_all(outgoing, ('fsdp', 'tp'), 0, 0, tiled=True)  62.7 us
    pallas_call x1, Pallas kernels, quantize_blocks(): pl.pallas_call(quantize_kernel, grid_spec=pltpu.PrefetchScalarGridSpec(nu...  18.6 us
    pallas_call x1, Pallas kernels, place_columns(): pl.pallas_call(place_kernel, grid=(SHARDS,), in_specs=[pl.BlockSpec((SHAR...  16.7 us
    pallas_call x1, Pallas kernels, local_rotation(): pl.pallas_call(local_kernel, grid=(steps,), in_specs=[pl.BlockSpec((rows,...  10.6 us

profile of v1, /device:TPU:6, one launch (start us, length us, event | category | flops | bytes accessed | tf_op | source)
XLA Modules:
  0.0 210.0 jit_solution(1468418185730243110)
XLA Ops:
  0.6 10.6 %local_rotation.1 = bf16[2,8,8,128,128]{4,3,2,1,0:T(8,128)(2,1)} custom-call(f32[1024,2048]{1,0:T(8,128)} %w_ref.1), custom_call_target="tpu_custom_call" | custom-call | tf_op jit(solution)/shard_map/local_rotation/pallas_call | solution.py:100
  11.2 62.7 %all_to_all.10 = bf16[128,128,128]{2,1,0:T(8,128)(2,1)} all-to-all(bf16[128,128,128]{2,1,0:T(8,128)(2,1)} %bitcast.2), channel_id=1, replica_groups=mesh['fsdp'=16,'tp'=8] {'fsdp','tp'}, dimensions={0} | all-to-all | bytes 8388608 | tf_op jit(solution)/shard_map/all_to_all | solution.py:241
  73.9 18.6 %quantize_blocks.1 = bf16[16,2064,128]{2,1,0:T(8,128)(2,1)} custom-call(s32[128]{0:T(128)} %owner_ref.1, bf16[16,8,128,128]{3,2,1,0:T(8,128)(2,1)} %bitcast.3), custom_call_target="tpu_custom_call" | custom-call | tf_op jit(solution)/shard_map/quantize_blocks/pallas_call | solution.py:175
  92.5 100.7 %all_to_all.11.in_ref.scale_in_ref = bf16[16,2064,128]{2,1,0:T(8,128)(2,1)} all-to-all(bf16[16,2064,128]{2,1,0:T(8,128)(2,1)} %quantize_blocks.1), channel_id=1, replica_groups=mesh['fsdp'=16,'tp'=8] {'fsdp'}, dimensions={0} | all-to-all | bytes 16908288 | tf_op jit(solution)/shard_map/all_to_all | solution.py:244
  193.2 16.7 %place_columns.1 = (bf16[2048,2048]{1,0:T(8,128)(2,1)}, bf16[16,2048]{1,0:T(8,128)(2,1)}) custom-call(bf16[16,2064,128]{2,1,0:T(8,128)(2,1)} %all_to_all.11.in_ref.scale_in_ref, bf16[16,2064,128]{2,1,0:T(8,128)(2,1)} %all_to_all.11.in_ref.scale_in_ref), custom_call_target="tpu_custom_call" | custom-call | tf_op jit(solution)/shard_map/place_columns/pallas_call | solution.py:220

commit v2 on v0

v2 whole, which is shorter than its diff:
```python
import functools

import jax
import jax.numpy as jnp
from jax import lax
from jax.experimental import pallas as pl
from jax.experimental.pallas import tpu as pltpu
from jax.sharding import PartitionSpec as P

BLOCK = 128
LANES = 128
GROUP = 16
EIGHT = 8
SHARDS = 16
TILES = 4
PAIRS = 4
STEP_SLOTS = 4
F32 = jnp.float32
BF16 = jnp.bfloat16


def butterflies(values):
    values = list(values)
    span = 1
    while span < len(values):
        for base in range(0, len(values), 2 * span):
            for k in range(base, base + span):
                low, high = values[k], values[k + span]
                values[k], values[k + span] = low + high, low - high
        span *= 2
    return values


def parity_signs(bits, scale):
    shift = 4
    while shift:
        bits = bits ^ (bits >> shift)
        shift //= 2
    return jnp.where((bits & 1) == 0, scale, -scale).astype(BF16)


def identity(size):
    row = lax.broadcasted_iota(jnp.int32, (size, size), 0)
    col = lax.broadcasted_iota(jnp.int32, (size, size), 1)
    return jnp.where(row == col, 1.0, 0.0).astype(BF16)


def transposed(eye, value):
    return lax.dot_general(
        eye, value, (((1,), (1,)), ((), ())), preferred_element_type=F32
    ).astype(BF16)


def local_kernel(w_ref, out_ref, sign_ref, eye_ref):
    @pl.when(pl.program_id(0) == 0)
    def _():
        row = lax.broadcasted_iota(jnp.int32, (256, 256), 0)
        col = lax.broadcasted_iota(jnp.int32, (256, 256), 1)
        sign_ref[...] = parity_signs(row & col, 1.0 / 32.0)
        eye_ref[...] = identity(256)

    for pair in range(TILES // 2):
        lanes = slice(2 * pair * LANES, 2 * (pair + 1) * LANES)
        mixed = butterflies([w_ref[256 * q : 256 * (q + 1), lanes] for q in range(4)])
        for q in range(4):
            turned = transposed(eye_ref[...], mixed[q].astype(BF16))
            half = jnp.dot(turned, sign_ref[...], preferred_element_type=F32).astype(BF16)
            for tile in range(2):
                for g in range(EIGHT):
                    row = (tile * EIGHT + g) * GROUP
                    for side in range(2):
                        out_ref[0, g, 2 * pair + tile, 2 * q + side] = half[
                            row : row + GROUP, side * BLOCK : (side + 1) * BLOCK
                        ]


def local_rotation(weights):
    rows, cols = weights.shape
    steps = cols // (TILES * LANES)
    per_half = steps // 2
    return pl.pallas_call(
        local_kernel,
        grid=(steps,),
        in_specs=[pl.BlockSpec((rows, TILES * LANES), lambda s: (0, s))],
        out_specs=pl.BlockSpec(
            (1, EIGHT, TILES, EIGHT, GROUP, BLOCK),
            lambda s: (s // per_half, 0, s % per_half, 0, 0, 0),
        ),
        out_shape=jax.ShapeDtypeStruct((2, EIGHT, EIGHT, EIGHT, GROUP, BLOCK), BF16),
        scratch_shapes=[pltpu.VMEM((256, 256), BF16), pltpu.VMEM((256, 256), BF16)],
        name="local_rotation",
    )(weights)


def quantize_kernel(
    owner_ref, in_ref, out_ref,
    received, held, sign_ref, block_scales, slot_scales, tail,
    in_sems, out_sem, tail_sem,
):
    def fetch(pair):
        return pltpu.make_async_copy(
            in_ref.at[:, pl.ds(2 * pair, 2)], received.at[pair], in_sems.at[pair]
        )

    for pair in range(PAIRS):
        fetch(pair).start()

    slot_scales[...] = jnp.zeros_like(slot_scales)
    row = lax.broadcasted_iota(jnp.int32, (256, 256), 0)
    col = lax.broadcasted_iota(jnp.int32, (256, 256), 1)
    signs = parity_signs((row // GROUP) & (col // GROUP), 0.25)
    same = (row & (GROUP - 1)) == (col & (GROUP - 1))
    sign_ref[...] = jnp.where(same, signs.astype(F32), 0.0).astype(BF16)

    @pl.loop(0, PAIRS)
    def _(pair):
        fetch(pair).wait()
        lane = lax.broadcasted_iota(jnp.int32, (SHARDS * GROUP, LANES), 1)
        for t in range(EIGHT):
            stacked = jnp.concatenate(
                [
                    jnp.concatenate(
                        [received[pair, a * EIGHT + t, side] for a in range(SHARDS)], axis=0
                    )
                    for side in range(2)
                ],
                axis=1,
            )
            mixed = jnp.dot(sign_ref[...], stacked, preferred_element_type=F32)
            for side in range(2):
                value = mixed[:, side * BLOCK : (side + 1) * BLOCK]
                largest = jnp.max(jnp.abs(value), axis=1, keepdims=True)
                scale = (largest + 1e-06).astype(BF16).astype(F32)
                ratio = (value * (1.0 / scale)).astype(BF16)
                pltpu.store(
                    block_scales.at[side],
                    jnp.broadcast_to(scale, lane.shape),
                    mask=lane // GROUP == t,
                )
                for a in range(SHARDS):
                    held[2 * pair + side, a, t * GROUP : (t + 1) * GROUP, :] = ratio[
                        a * GROUP : (a + 1) * GROUP
                    ]
        slot_lane = lane[:GROUP] & (GROUP - 1)
        for side in range(2):
            for a in range(SHARDS):
                rank = owner_ref[a * EIGHT + 2 * pair + side]
                pltpu.make_async_copy(
                    held.at[2 * pair + side, a],
                    out_ref.at[rank, pl.ds(a * BLOCK, BLOCK)],
                    out_sem,
                ).start()
                pltpu.store(
                    slot_scales.at[rank],
                    block_scales[side, a * GROUP : (a + 1) * GROUP, :],
                    mask=slot_lane == a,
                )

    tail[...] = slot_scales[...].astype(BF16)
    tail_copy = pltpu.make_async_copy(
        tail, out_ref.at[:, pl.ds(SHARDS * BLOCK, GROUP), :], tail_sem
    )
    tail_copy.start()
    pltpu.make_async_copy(held, held, out_sem).wait()
    tail_copy.wait()


def quantize_blocks(owner, received):
    out_rows = SHARDS * BLOCK + GROUP
    sources = received.shape[0]
    return pl.pallas_call(
        quantize_kernel,
        in_specs=[
            pl.BlockSpec(memory_space=pltpu.SMEM),
            pl.BlockSpec(memory_space=pl.ANY),
        ],
        out_specs=pl.BlockSpec(memory_space=pl.ANY),
        scratch_shapes=[
            pltpu.VMEM((PAIRS, sources, 2, GROUP, BLOCK), BF16),
            pltpu.VMEM((EIGHT, SHARDS, BLOCK, BLOCK), BF16),
            pltpu.VMEM((256, 256), BF16),
            pltpu.VMEM((2, SHARDS * GROUP, LANES), F32),
            pltpu.VMEM((SHARDS, GROUP, LANES), F32),
            pltpu.VMEM((SHARDS, GROUP, LANES), BF16),
            pltpu.SemaphoreType.DMA((PAIRS,)),
            pltpu.SemaphoreType.DMA,
            pltpu.SemaphoreType.DMA,
        ],
        out_shape=jax.ShapeDtypeStruct((SHARDS, out_rows, LANES), BF16),
        name="quantize_blocks",
    )(owner, received)


def place_kernel(
    rank_ref, owner_ref, in_ref, scale_in_ref, out_ref, scale_out_ref, eye_ref
):
    @pl.when(pl.program_id(0) == 0)
    def _():
        eye_ref[...] = identity(BLOCK)
        stacked = jnp.concatenate([scale_in_ref[m] for m in range(SHARDS)], axis=0)
        by_column = transposed(eye_ref[...], stacked)
        for t in range(EIGHT):
            scale_out_ref[:, t * 2 * LANES : (t + 1) * 2 * LANES] = by_column[
                t * GROUP : (t + 1) * GROUP
            ]

    for slot in range(STEP_SLOTS):
        rows = slice(slot * BLOCK, (slot + 1) * BLOCK)
        first = (pl.program_id(0) * STEP_SLOTS + slot) * EIGHT
        taken = functools.reduce(
            jnp.logical_or, [owner_ref[first + j] == rank_ref[0] for j in range(EIGHT)]
        )

        @pl.when(taken)
        def _():
            for t in range(EIGHT):
                row = slot * BLOCK + t * GROUP
                stacked = jnp.concatenate(
                    [in_ref[m, row : row + GROUP, :] for m in range(SHARDS)], axis=0
                )
                out_ref[rows, t * 2 * LANES : (t + 1) * 2 * LANES] = transposed(
                    eye_ref[...], stacked
                )

        @pl.when(jnp.logical_not(taken))
        def _():
            out_ref[rows, :] = jnp.zeros((BLOCK, out_ref.shape[1]), BF16)


def place_columns(owner, incoming):
    cols = SHARDS * LANES
    step_rows = STEP_SLOTS * BLOCK
    rank = lax.axis_index("fsdp").astype(jnp.int32).reshape(1)
    return pl.pallas_call(
        place_kernel,
        grid=(SHARDS // STEP_SLOTS,),
        in_specs=[
            pl.BlockSpec(memory_space=pltpu.SMEM),
            pl.BlockSpec(memory_space=pltpu.SMEM),
            pl.BlockSpec((SHARDS, step_rows, LANES), lambda s: (0, s, 0)),
            pl.BlockSpec((SHARDS, SHARDS, LANES), lambda s: (0, BLOCK, 0)),
        ],
        out_specs=[
            pl.BlockSpec((step_rows, cols), lambda s: (s, 0)),
            pl.BlockSpec((SHARDS, cols), lambda s: (0, 0)),
        ],
        out_shape=[
            jax.ShapeDtypeStruct((SHARDS * BLOCK, cols), BF16),
            jax.ShapeDtypeStruct((SHARDS, cols), BF16),
        ],
        scratch_shapes=[pltpu.VMEM((BLOCK, BLOCK), BF16)],
        name="place_columns",
    )(rank, owner, incoming, incoming)


def per_device(weights, owner):
    outgoing = local_rotation(weights).reshape(SHARDS * EIGHT, EIGHT * GROUP, BLOCK)
    received = lax.all_to_all(outgoing, ("fsdp", "tp"), 0, 0, tiled=True)
    received = received.reshape(SHARDS * EIGHT, EIGHT, GROUP, BLOCK)
    slotted = quantize_blocks(owner, received)
    incoming = lax.all_to_all(slotted, "fsdp", 0, 0, tiled=True)
    return tuple(place_columns(owner, incoming))


def solution(mesh):
    return jax.shard_map(
        per_device,
        mesh=mesh,
        in_specs=(P("fsdp", "tp"), P()),
        out_specs=(P("fsdp", "tp"), P("fsdp", "tp")),
        check_vma=False,
    )
```

time: 1120 us -> 241 us (0.22)
  waiting for transfers between devices: 915 us -> 146 us
  local copies, waits for them, and re-layouts: 66.6 us -> 0 us
  blocking collectives: 0 us -> 62.7 us
  matrix products: 58.8 us -> 0 us
  other arithmetic: 46.6 us -> 0 us
  starting transfers between devices: 31.6 us -> 6.54 us
  Pallas kernels: 0 us -> 23 us
    ppermute x4 -> x0, waiting for transfers between devices: 721 us -> none  [swapped(): return lax.ppermute(value, axis, pairs)]
    all_to_all x0 -> x1, blocking collectives: none -> 62.7 us  [per_device(): received = lax.all_to_all(outgoing, ('fsdp', 'tp'), 0, 0, tiled=True)]
    dot_general x3 -> x0, matrix products: 58.8 us -> none  [the longest x1 47.3 us: per_device(): rotated = jnp.dot(signs_table(row_count), weights, precision=highest)]
    all_to_all x4 -> x1, waiting for transfers between devices: 194 us -> 146 us  [per_device(): incoming = lax.all_to_all(slotted, 'fsdp', 0, 0, tiled=True)]
    select_n x3 -> x0, other arithmetic: 36.2 us -> none  [per_device(): rotated = jnp.where(lower_half, rotated + partner, partner - rotated)]
    unnamed x6 -> x0, local copies, waits for them, and re-layouts: 31.4 us -> none
    pallas_call x0 -> x3, Pallas kernels: none -> 23 us  [the longest x1 8.6 us: place_columns(): pl.pallas_call(place_kernel, grid=(SHARDS // STEP_SLOTS,), in_specs=[pl.B...]
    reshape x3 -> x0, local copies, waits for them, and re-layouts: 21.8 us -> none  [the longest x1 13 us: per_device(): outgoing.reshape(fsdp_size, pair_slots * BLOCK, col_tiles, tp_size, TILE)]
  transfers between devices with their start and end apart: 8 -> 1, of which waited for: 6 -> 1; matrix products, arithmetic and copies ran while one was open for 4% -> 0% of each run, Pallas kernels for 0% -> 0%
where the time goes in v2:
time: 241 us; the launch traced here: 239 us
  waiting for transfers between devices  146 us (61%)
  blocking collectives  62.7 us (26%)
  Pallas kernels  23 us (10%)
  starting transfers between devices  6.54 us (3%)
    all_to_all x1, waiting for transfers between devices, per_device(): incoming = lax.all_to_all(slotted, 'fsdp', 0, 0, tiled=True)  146 us
    all_to_all x1, blocking collectives, per_device(): received = lax.all_to_all(outgoing, ('fsdp', 'tp'), 0, 0, tiled=True)  62.7 us
    pallas_call x1, Pallas kernels, place_columns(): pl.pallas_call(place_kernel, grid=(SHARDS // STEP_SLOTS,), in_specs=[pl.B...  8.6 us
    pallas_call x1, Pallas kernels, local_rotation(): pl.pallas_call(local_kernel, grid=(steps,), in_specs=[pl.BlockSpec((rows,...  7.93 us
    all_to_all x1, starting transfers between devices, per_device(): incoming = lax.all_to_all(slotted, 'fsdp', 0, 0, tiled=True)  6.54 us
    pallas_call x1, Pallas kernels, quantize_blocks(): pl.pallas_call(quantize_kernel, in_specs=[pl.BlockSpec(memory_space=pltpu...  6.49 us
  transfers between devices with their start and end apart: 1, of which 1 were waited for; matrix products, arithmetic and copies ran while one was open for 0% of the time, Pallas kernels for 0%

profile of v2, /device:TPU:6, one launch (start us, length us, event | category | flops | bytes accessed | tf_op | source)
XLA Modules:
  0.0 239.1 jit_solution(16999035394968396219)
XLA Ops:
  0.6 7.9 %local_rotation.1 = bf16[2,8,8,8,16,128]{5,4,3,2,1,0:T(8,128)(2,1)} custom-call(f32[1024,2048]{1,0:T(8,128)} %w_ref.1), custom_call_target="tpu_custom_call" | custom-call | tf_op jit(solution)/shard_map/local_rotation/pallas_call | solution.py:81
  8.6 62.7 %all_to_all.10 = bf16[128,128,128]{2,1,0:T(8,128)(2,1)} all-to-all(bf16[128,128,128]{2,1,0:T(8,128)(2,1)} %bitcast.3), channel_id=1, replica_groups=mesh['fsdp'=16,'tp'=8] {'fsdp','tp'}, dimensions={0} | all-to-all | bytes 8388608 | tf_op jit(solution)/shard_map/all_to_all | solution.py:258
  71.3 6.5 %quantize_blocks.1 = bf16[16,2064,128]{2,1,0:T(8,128)(2,1)} custom-call(s32[128]{0:T(128)} %owner_ref.3, bf16[128,8,16,128]{3,2,1,0:T(8,128)(2,1)} %bitcast.4), custom_call_target="tpu_custom_call" | custom-call | tf_op jit(solution)/shard_map/quantize_blocks/pallas_call | solution.py:171
  77.8 6.5 %all-to-all-start.1 = ((bf16[16,2064,128]{2,1,0:T(8,128)(2,1)}), bf16[16,2064,128]{2,1,0:T(8,128)(2,1)}, u32[]{:S(2)}, u32[]{:S(2)}) async-start(bf16[16,2064,128]{2,1,0:T(8,128)(2,1)} %quantize_blocks.1), calls=%async_computation.1 | async-start | bytes 16908288 | tf_op jit(solution)/shard_map/all_to_all | solution.py:261
  84.3 146.2 %all-to-all-done.1.in_ref.scale_in_ref = bf16[16,2064,128]{2,1,0:T(8,128)(2,1)} async-done(((bf16[16,2064,128]{2,1,0:T(8,128)(2,1)}), bf16[16,2064,128]{2,1,0:T(8,128)(2,1)}, u32[]{:S(2)}, u32[]{:S(2)}) %all-to-all-start.1) | async-done | bytes 8454176 | tf_op jit(solution)/shard_map/all_to_all | solution.py:261
  230.5 8.6 %place_columns.1 = (bf16[2048,2048]{1,0:T(8,128)(2,1)}, bf16[16,2048]{1,0:T(8,128)(2,1)}) custom-call(s32[1]{0:T(128)} %bitcast.rank_ref, s32[128]{0:T(128)} %owner_ref.3, bf16[16,2064,128]{2,1,0:T(8,128)(2,1)} %all-to-all-done.1.in_ref.scale_in_ref, bf16[16,2064,128]{2,1,0:T(8,128)(2,1)} %all-to-all-done.1.in_ref.scale_in_ref), custom_call_target="tpu_custom_call" | custom-call | tf_op jit(solution)/shard_map/place_columns/pallas_call | solution.py:234
Async XLA Ops:
  77.8 152.8 %all-to-all-start.1 = ((bf16[16,2064,128]{2,1,0:T(8,128)(2,1)}), bf16[16,2064,128]{2,1,0:T(8,128)(2,1)}, u32[]{:S(2)}, u32[]{:S(2)}) async-start(bf16[16,2064,128]{2,1,0:T(8,128)(2,1)} %quantize_blocks.1), calls=%async_computation.1 | async-start | bytes 16908288 | tf_op jit(solution)/shard_map/all_to_all | solution.py:261

commit v3 on v2

--- a/solution.py
+++ b/solution.py
@@ -192,7 +192,7 @@
 
 
 def place_kernel(
-    rank_ref, owner_ref, in_ref, scale_in_ref, out_ref, scale_out_ref, eye_ref
+    owner_ref, in_ref, scale_in_ref, out_ref, scale_out_ref, eye_ref
 ):
     @pl.when(pl.program_id(0) == 0)
     def _():
@@ -204,11 +204,12 @@
                 t * GROUP : (t + 1) * GROUP
             ]
 
+    rank = lax.axis_index("fsdp")
     for slot in range(STEP_SLOTS):
         rows = slice(slot * BLOCK, (slot + 1) * BLOCK)
         first = (pl.program_id(0) * STEP_SLOTS + slot) * EIGHT
         taken = functools.reduce(
-            jnp.logical_or, [owner_ref[first + j] == rank_ref[0] for j in range(EIGHT)]
+            jnp.logical_or, [owner_ref[first + j] == rank for j in range(EIGHT)]
         )
 
         @pl.when(taken)
@@ -230,13 +231,11 @@
 def place_columns(owner, incoming):
     cols = SHARDS * LANES
     step_rows = STEP_SLOTS * BLOCK
-    rank = lax.axis_index("fsdp").astype(jnp.int32).reshape(1)
     return pl.pallas_call(
         place_kernel,
         grid=(SHARDS // STEP_SLOTS,),
         in_specs=[
             pl.BlockSpec(memory_space=pltpu.SMEM),
-            pl.BlockSpec(memory_space=pltpu.SMEM),
             pl.BlockSpec((SHARDS, step_rows, LANES), lambda s: (0, s, 0)),
             pl.BlockSpec((SHARDS, SHARDS, LANES), lambda s: (0, BLOCK, 0)),
         ],
@@ -250,7 +249,7 @@
         ],
         scratch_shapes=[pltpu.VMEM((BLOCK, BLOCK), BF16)],
         name="place_columns",
-    )(rank, owner, incoming, incoming)
+    )(owner, incoming, incoming)
 
 
 def per_device(weights, owner):

time: 241 us -> 189 us (0.78)
  waiting for transfers between devices: 146 us -> 0 us
  blocking collectives: 62.7 us -> 163 us
  starting transfers between devices: 6.54 us -> 0 us
    all_to_all x1 -> x0, waiting for transfers between devices: 146 us -> none  [per_device(): incoming = lax.all_to_all(slotted, 'fsdp', 0, 0, tiled=True)]
    all_to_all x0 -> x1, blocking collectives: none -> 101 us  [per_device(): incoming = lax.all_to_all(slotted, 'fsdp', 0, 0, tiled=True)]
    all_to_all x1 -> x0, starting transfers between devices: 6.54 us -> none  [per_device(): incoming = lax.all_to_all(slotted, 'fsdp', 0, 0, tiled=True)]
  transfers between devices with their start and end apart: 1 -> 0, of which waited for: 1 -> 0; matrix products, arithmetic and copies ran while one was open for 0% -> 0% of each run, Pallas kernels for 0% -> 0%
where the time goes in v3:
time: 189 us; the launch traced here: 187 us
  blocking collectives  163 us (86%)
  Pallas kernels  23.2 us (12%)
    all_to_all x1, blocking collectives, per_device(): incoming = lax.all_to_all(slotted, 'fsdp', 0, 0, tiled=True)  101 us
    all_to_all x1, blocking collectives, per_device(): received = lax.all_to_all(outgoing, ('fsdp', 'tp'), 0, 0, tiled=True)  62.7 us
    pallas_call x1, Pallas kernels, place_columns(): pl.pallas_call(place_kernel, grid=(SHARDS // STEP_SLOTS,), in_specs=[pl.B...  8.81 us
    pallas_call x1, Pallas kernels, local_rotation(): pl.pallas_call(local_kernel, grid=(steps,), in_specs=[pl.BlockSpec((rows,...  7.93 us
    pallas_call x1, Pallas kernels, quantize_blocks(): pl.pallas_call(quantize_kernel, in_specs=[pl.BlockSpec(memory_space=pltpu...  6.49 us

profile of v3, /device:TPU:6, one launch (start us, length us, event | category | flops | bytes accessed | tf_op | source)
XLA Modules:
  0.0 187.3 jit_solution(3347958289197030547)
XLA Ops:
  0.6 7.9 %local_rotation.1 = bf16[2,8,8,8,16,128]{5,4,3,2,1,0:T(8,128)(2,1)} custom-call(f32[1024,2048]{1,0:T(8,128)} %w_ref.1), custom_call_target="tpu_custom_call" | custom-call | tf_op jit(solution)/shard_map/local_rotation/pallas_call | solution.py:81
  8.6 62.7 %all_to_all.10 = bf16[128,128,128]{2,1,0:T(8,128)(2,1)} all-to-all(bf16[128,128,128]{2,1,0:T(8,128)(2,1)} %bitcast.2), channel_id=1, replica_groups=mesh['fsdp'=16,'tp'=8] {'fsdp','tp'}, dimensions={0} | all-to-all | bytes 8388608 | tf_op jit(solution)/shard_map/all_to_all | solution.py:257
  71.3 6.5 %quantize_blocks.1 = bf16[16,2064,128]{2,1,0:T(8,128)(2,1)} custom-call(s32[128]{0:T(128)} %owner_ref.3, bf16[128,8,16,128]{3,2,1,0:T(8,128)(2,1)} %bitcast.3), custom_call_target="tpu_custom_call" | custom-call | tf_op jit(solution)/shard_map/quantize_blocks/pallas_call | solution.py:171
  77.8 100.7 %all_to_all.11.in_ref.scale_in_ref = bf16[16,2064,128]{2,1,0:T(8,128)(2,1)} all-to-all(bf16[16,2064,128]{2,1,0:T(8,128)(2,1)} %quantize_blocks.1), channel_id=1, replica_groups=mesh['fsdp'=16,'tp'=8] {'fsdp'}, dimensions={0} | all-to-all | bytes 16908288 | tf_op jit(solution)/shard_map/all_to_all | solution.py:260
  178.5 8.8 %place_columns.1 = (bf16[2048,2048]{1,0:T(8,128)(2,1)}, bf16[16,2048]{1,0:T(8,128)(2,1)}) custom-call(s32[128]{0:T(128)} %owner_ref.3, bf16[16,2064,128]{2,1,0:T(8,128)(2,1)} %all_to_all.11.in_ref.scale_in_ref, bf16[16,2064,128]{2,1,0:T(8,128)(2,1)} %all_to_all.11.in_ref.scale_in_ref), custom_call_target="tpu_custom_call" | custom-call | tf_op jit(solution)/shard_map/place_columns/pallas_call | solution.py:234

commit v4 on v3

--- a/solution.py
+++ b/solution.py
@@ -15,6 +15,9 @@
 TILES = 4
 PAIRS = 4
 STEP_SLOTS = 4
+SIDE = 4
+PACKED = 12
+META_RANK, META_POS, META_SLOT, META_HOT, META_FITS, META_OWNER = range(6)
 F32 = jnp.float32
 BF16 = jnp.bfloat16
 
@@ -51,13 +54,61 @@
     ).astype(BF16)
 
 
-def local_kernel(w_ref, out_ref, sign_ref, eye_ref):
+def fill_tables(owner_row, me, meta_ref):
+    shape = (BLOCK, BLOCK)
+    by_lane = jnp.broadcast_to(owner_row.astype(F32), shape)
+    by_row = by_lane.T
+    row = lax.broadcasted_iota(jnp.int32, shape, 0)
+    lane = lax.broadcasted_iota(jnp.int32, shape, 1)
+    equal = by_lane == by_row
+
+    def count(mask, axis):
+        total = jnp.sum(jnp.where(mask, 1.0, 0.0), axis=axis, keepdims=True)
+        return total.astype(jnp.int32)
+
+    total = count(equal, 0)
+    position = count(equal & (row < lane), 0)
+    position_by_row = count(equal & (lane < row), 1)
+    hot = jnp.max(jnp.where(total == SHARDS, owner_row, -1), axis=1, keepdims=True)
+    x, z = hot >> 2, hot & (SIDE - 1)
+    around = [
+        (((x + 1) & (SIDE - 1)) << 2) | z,
+        (((x - 1) & (SIDE - 1)) << 2) | z,
+        (x << 2) | ((z + 1) & (SIDE - 1)),
+        (x << 2) | ((z - 1) & (SIDE - 1)),
+    ]
+    is_hot = owner_row == hot
+    is_near = functools.reduce(jnp.logical_or, [owner_row == near for near in around])
+    load = jnp.where(is_hot, 0, total + is_near.astype(jnp.int32))
+    fits = (jnp.max(load, axis=1, keepdims=True) <= PACKED) & (hot >= 0)
+    fits = jnp.broadcast_to(fits.astype(jnp.int32), owner_row.shape) != 0
+    over = is_hot & (position >= PACKED) & fits
+    rank = owner_row
+    for d, near in enumerate(around):
+        rank = jnp.where(over & (position == PACKED + d), near, rank)
+    block = lane[:1]
+    position = jnp.where(fits, jnp.where(over, PACKED - 1, position), block >> 3)
+    mine = (by_row == me.astype(F32)) & ((row >> 3) == lane)
+    slot = jnp.sum(
+        jnp.where(mine, (position_by_row + 1).astype(F32), 0.0), axis=0, keepdims=True
+    ).astype(jnp.int32) - 1
+    slot = jnp.where(fits | (slot < 0), slot, block)
+    meta_ref[META_RANK : META_RANK + 1, :] = rank
+    meta_ref[META_POS : META_POS + 1, :] = position
+    meta_ref[META_SLOT : META_SLOT + 1, :] = slot
+    meta_ref[META_HOT : META_HOT + 1, :] = jnp.broadcast_to(hot, owner_row.shape)
+    meta_ref[META_FITS : META_FITS + 1, :] = fits.astype(jnp.int32)
+    meta_ref[META_OWNER : META_OWNER + 1, :] = owner_row
+
+
+def local_kernel(owner_ref, w_ref, out_ref, meta_ref, sign_ref, eye_ref):
     @pl.when(pl.program_id(0) == 0)
     def _():
         row = lax.broadcasted_iota(jnp.int32, (256, 256), 0)
         col = lax.broadcasted_iota(jnp.int32, (256, 256), 1)
         sign_ref[...] = parity_signs(row & col, 1.0 / 32.0)
         eye_ref[...] = identity(256)
+        fill_tables(owner_ref[...], lax.axis_index("fsdp"), meta_ref)
 
     for pair in range(TILES // 2):
         lanes = slice(2 * pair * LANES, 2 * (pair + 1) * LANES)
@@ -74,26 +125,35 @@
                         ]
 
 
-def local_rotation(weights):
+def local_rotation(owner, weights):
     rows, cols = weights.shape
     steps = cols // (TILES * LANES)
     per_half = steps // 2
     return pl.pallas_call(
         local_kernel,
         grid=(steps,),
-        in_specs=[pl.BlockSpec((rows, TILES * LANES), lambda s: (0, s))],
-        out_specs=pl.BlockSpec(
-            (1, EIGHT, TILES, EIGHT, GROUP, BLOCK),
-            lambda s: (s // per_half, 0, s % per_half, 0, 0, 0),
-        ),
-        out_shape=jax.ShapeDtypeStruct((2, EIGHT, EIGHT, EIGHT, GROUP, BLOCK), BF16),
+        in_specs=[
+            pl.BlockSpec((1, BLOCK), lambda s: (0, 0)),
+            pl.BlockSpec((rows, TILES * LANES), lambda s: (0, s)),
+        ],
+        out_specs=[
+            pl.BlockSpec(
+                (1, EIGHT, TILES, EIGHT, GROUP, BLOCK),
+                lambda s: (s // per_half, 0, s % per_half, 0, 0, 0),
+            ),
+            pl.BlockSpec((EIGHT, BLOCK), lambda s: (0, 0)),
+        ],
+        out_shape=[
+            jax.ShapeDtypeStruct((2, EIGHT, EIGHT, EIGHT, GROUP, BLOCK), BF16),
+            jax.ShapeDtypeStruct((EIGHT, BLOCK), jnp.int32),
+        ],
         scratch_shapes=[pltpu.VMEM((256, 256), BF16), pltpu.VMEM((256, 256), BF16)],
         name="local_rotation",
-    )(weights)
+    )(owner.reshape(1, BLOCK), weights)
 
 
 def quantize_kernel(
-    owner_ref, in_ref, out_ref,
+    meta_ref, in_ref, out_ref,
     received, held, sign_ref, block_scales, slot_scales, tail,
     in_sems, out_sem, tail_sem,
 ):
@@ -144,29 +204,30 @@
         slot_lane = lane[:GROUP] & (GROUP - 1)
         for side in range(2):
             for a in range(SHARDS):
-                rank = owner_ref[a * EIGHT + 2 * pair + side]
+                block = a * EIGHT + 2 * pair + side
+                start = pl.multiple_of(meta_ref[META_POS, block] * BLOCK, BLOCK)
                 pltpu.make_async_copy(
                     held.at[2 * pair + side, a],
-                    out_ref.at[rank, pl.ds(a * BLOCK, BLOCK)],
+                    out_ref.at[meta_ref[META_RANK, block], pl.ds(start, BLOCK)],
                     out_sem,
                 ).start()
                 pltpu.store(
-                    slot_scales.at[rank],
+                    slot_scales.at[meta_ref[META_OWNER, block]],
                     block_scales[side, a * GROUP : (a + 1) * GROUP, :],
                     mask=slot_lane == a,
                 )
 
     tail[...] = slot_scales[...].astype(BF16)
     tail_copy = pltpu.make_async_copy(
-        tail, out_ref.at[:, pl.ds(SHARDS * BLOCK, GROUP), :], tail_sem
+        tail, out_ref.at[:, pl.ds(out_ref.shape[1] - GROUP, GROUP), :], tail_sem
     )
     tail_copy.start()
     pltpu.make_async_copy(held, held, out_sem).wait()
     tail_copy.wait()
 
 
-def quantize_blocks(owner, received):
-    out_rows = SHARDS * BLOCK + GROUP
+def quantize_blocks(meta, received, capacity):
+    out_rows = capacity * BLOCK + GROUP
     sources = received.shape[0]
     return pl.pallas_call(
         quantize_kernel,
@@ -188,12 +249,20 @@
         ],
         out_shape=jax.ShapeDtypeStruct((SHARDS, out_rows, LANES), BF16),
         name="quantize_blocks",
-    )(owner, received)
-
-
-def place_kernel(
-    owner_ref, in_ref, scale_in_ref, out_ref, scale_out_ref, eye_ref
-):
+    )(meta, received)
+
+
+def place_block(eye, source, target):
+    for t in range(EIGHT):
+        stacked = jnp.concatenate(
+            [source[m, t * GROUP : (t + 1) * GROUP, :] for m in range(SHARDS)], axis=0
+        )
+        target[:, t * 2 * LANES : (t + 1) * 2 * LANES] = transposed(eye, stacked)
+
+
+def place_kernel(capacity, meta_ref, *refs):
+    ins, (scale_in_ref, out_ref, scale_out_ref, eye_ref) = refs[:STEP_SLOTS], refs[STEP_SLOTS:]
+
     @pl.when(pl.program_id(0) == 0)
     def _():
         eye_ref[...] = identity(BLOCK)
@@ -204,61 +273,151 @@
                 t * GROUP : (t + 1) * GROUP
             ]
 
-    rank = lax.axis_index("fsdp")
-    for slot in range(STEP_SLOTS):
-        rows = slice(slot * BLOCK, (slot + 1) * BLOCK)
-        first = (pl.program_id(0) * STEP_SLOTS + slot) * EIGHT
-        taken = functools.reduce(
-            jnp.logical_or, [owner_ref[first + j] == rank for j in range(EIGHT)]
-        )
+    for k in range(STEP_SLOTS):
+        target = out_ref.at[pl.ds(k * BLOCK, BLOCK), :]
+        source = meta_ref[META_SLOT, pl.program_id(0) * STEP_SLOTS + k]
+        taken = (source >= 0) & (source < capacity)
 
         @pl.when(taken)
         def _():
-            for t in range(EIGHT):
-                row = slot * BLOCK + t * GROUP
-                stacked = jnp.concatenate(
-                    [in_ref[m, row : row + GROUP, :] for m in range(SHARDS)], axis=0
-                )
-                out_ref[rows, t * 2 * LANES : (t + 1) * 2 * LANES] = transposed(
-                    eye_ref[...], stacked
-                )
+            place_block(eye_ref[...], ins[k], target)
 
         @pl.when(jnp.logical_not(taken))
         def _():
-            out_ref[rows, :] = jnp.zeros((BLOCK, out_ref.shape[1]), BF16)
-
-
-def place_columns(owner, incoming):
+            target[...] = jnp.zeros(target.shape, BF16)
+
+
+def place_columns(meta, incoming, capacity):
     cols = SHARDS * LANES
     step_rows = STEP_SLOTS * BLOCK
+
+    def slot_map(k):
+        def index(s, meta_ref):
+            source = meta_ref[META_SLOT, s * STEP_SLOTS + k]
+            return (0, jnp.clip(source, 0, capacity - 1), 0)
+
+        return index
+
     return pl.pallas_call(
-        place_kernel,
-        grid=(SHARDS // STEP_SLOTS,),
-        in_specs=[
-            pl.BlockSpec(memory_space=pltpu.SMEM),
-            pl.BlockSpec((SHARDS, step_rows, LANES), lambda s: (0, s, 0)),
-            pl.BlockSpec((SHARDS, SHARDS, LANES), lambda s: (0, BLOCK, 0)),
-        ],
-        out_specs=[
-            pl.BlockSpec((step_rows, cols), lambda s: (s, 0)),
-            pl.BlockSpec((SHARDS, cols), lambda s: (0, 0)),
-        ],
+        functools.partial(place_kernel, capacity),
+        grid_spec=pltpu.PrefetchScalarGridSpec(
+            num_scalar_prefetch=1,
+            grid=(SHARDS // STEP_SLOTS,),
+            in_specs=[
+                pl.BlockSpec((SHARDS, BLOCK, LANES), slot_map(k)) for k in range(STEP_SLOTS)
+            ]
+            + [pl.BlockSpec((SHARDS, GROUP, LANES), lambda s, _: (0, capacity * EIGHT, 0))],
+            out_specs=[
+                pl.BlockSpec((step_rows, cols), lambda s, _: (s, 0)),
+                pl.BlockSpec((SHARDS, cols), lambda s, _: (0, 0)),
+            ],
+            scratch_shapes=[pltpu.VMEM((BLOCK, BLOCK), BF16)],
+        ),
         out_shape=[
             jax.ShapeDtypeStruct((SHARDS * BLOCK, cols), BF16),
             jax.ShapeDtypeStruct((SHARDS, cols), BF16),
         ],
-        scratch_shapes=[pltpu.VMEM((BLOCK, BLOCK), BF16)],
+        cost_estimate=pl.CostEstimate(
+            flops=2 * SHARDS * BLOCK * BLOCK * cols,
+            bytes_accessed=4 * SHARDS * BLOCK * cols,
+            transcendentals=0,
+        ),
         name="place_columns",
-    )(owner, incoming, incoming)
+    )(meta, *[incoming] * (STEP_SLOTS + 1))
+
+
+def copy_kernel(in_ref, out_ref):
+    out_ref[...] = in_ref[...]
+
+
+def last_position(incoming):
+    shape = (SHARDS, BLOCK, LANES)
+    return pl.pallas_call(
+        copy_kernel,
+        grid=(1,),
+        in_specs=[pl.BlockSpec(shape, lambda s: (0, PACKED - 1, 0))],
+        out_specs=pl.BlockSpec(shape, lambda s: (0, 0, 0)),
+        out_shape=jax.ShapeDtypeStruct(shape, BF16),
+        name="last_position",
+    )(incoming)
+
+
+def patch_kernel(
+    meta_ref, near_0, near_1, near_2, near_3, _, out_ref, nears, buffers, eye_ref, in_sem, sem
+):
+    @pl.when(meta_ref[META_HOT, 0] == lax.axis_index("fsdp"))
+    def _():
+        loads = [
+            pltpu.make_async_copy(near, nears.at[d], in_sem.at[d])
+            for d, near in enumerate((near_0, near_1, near_2, near_3))
+        ]
+        for load in loads:
+            load.start()
+        eye_ref[...] = identity(BLOCK)
+        stores = []
+        for d, load in enumerate(loads):
+            load.wait()
+            place_block(eye_ref[...], nears.at[d], buffers.at[d])
+            stores.append(
+                pltpu.make_async_copy(
+                    buffers.at[d], out_ref.at[pl.ds((PACKED + d) * BLOCK, BLOCK), :], sem.at[d]
+                )
+            )
+            stores[-1].start()
+        for store in stores:
+            store.wait()
+
+
+def patch_hot_rank(meta, rolled, nears):
+    cols = rolled.shape[1]
+    return pl.pallas_call(
+        patch_kernel,
+        in_specs=[pl.BlockSpec(memory_space=pltpu.SMEM)]
+        + [pl.BlockSpec(memory_space=pl.ANY)] * 5,
+        out_specs=pl.BlockSpec(memory_space=pl.ANY),
+        out_shape=jax.ShapeDtypeStruct(rolled.shape, rolled.dtype),
+        scratch_shapes=[
+            pltpu.VMEM((4, SHARDS, BLOCK, LANES), BF16),
+            pltpu.VMEM((4, BLOCK, cols), BF16),
+            pltpu.VMEM((BLOCK, BLOCK), BF16),
+            pltpu.SemaphoreType.DMA((4,)),
+            pltpu.SemaphoreType.DMA((4,)),
+        ],
+        input_output_aliases={5: 0},
+        name="patch_hot_rank",
+    )(meta, *nears, rolled)
+
+
+def shifted(value, dx, dz):
+    pairs = []
+    for source in range(SHARDS):
+        x, z = divmod(source, SIDE)
+        pairs.append((source, (x + dx) % SIDE * SIDE + (z + dz) % SIDE))
+    return lax.ppermute(value, "fsdp", pairs)
+
+
+def general(meta, received):
+    slotted = quantize_blocks(meta, received, SHARDS)
+    incoming = lax.all_to_all(slotted, "fsdp", 0, 0, tiled=True)
+    return tuple(place_columns(meta, incoming, SHARDS))
+
+
+def packed(meta, received):
+    slotted = quantize_blocks(meta, received, PACKED)
+    incoming = lax.all_to_all(slotted, "fsdp", 0, 0, tiled=True)
+    foreign = last_position(incoming)
+    nears = [shifted(foreign, dx, dz) for dx, dz in ((-1, 0), (1, 0), (0, -1), (0, 1))]
+    rolled, rolled_scales = place_columns(meta, incoming, PACKED)
+    return patch_hot_rank(meta, rolled, nears), rolled_scales
 
 
 def per_device(weights, owner):
-    outgoing = local_rotation(weights).reshape(SHARDS * EIGHT, EIGHT * GROUP, BLOCK)
+    outgoing, meta = local_rotation(owner, weights)
+    outgoing = outgoing.reshape(SHARDS * EIGHT, EIGHT * GROUP, BLOCK)
     received = lax.all_to_all(outgoing, ("fsdp", "tp"), 0, 0, tiled=True)
     received = received.reshape(SHARDS * EIGHT, EIGHT, GROUP, BLOCK)
-    slotted = quantize_blocks(owner, received)
-    incoming = lax.all_to_all(slotted, "fsdp", 0, 0, tiled=True)
-    return tuple(place_columns(owner, incoming))
+    received, meta = lax.optimization_barrier((received, meta))
+    return lax.cond(meta[META_FITS, 0] != 0, packed, general, meta, received)
 
 
 def solution(mesh):

time: 189 us -> 181 us (0.958); the launches traced: 187 us -> 182 us
  blocking collectives: 163 us -> 141 us
  Pallas kernels: 23.2 us -> 29.5 us
  starting transfers between devices: 0 us -> 5.38 us
  waiting for transfers between devices: 0 us -> 3.29 us
    all_to_all x1, blocking collectives: 101 us -> 78.2 us  [packed(): incoming = lax.all_to_all(slotted, 'fsdp', 0, 0, tiled=True)]
    pallas_call x2 -> x4, Pallas kernels: 16.7 us -> 23 us  [the longest x1 9.09 us: place_columns(): pl.pallas_call(functools.partial(place_kernel, capacity), grid_spec=pltpu...]
    ppermute x0 -> x4, starting transfers between devices: none -> 5.38 us  [shifted(): return lax.ppermute(value, 'fsdp', pairs)]
    ppermute x0 -> x4, waiting for transfers between devices: none -> 3.29 us  [shifted(): return lax.ppermute(value, 'fsdp', pairs)]
  transfers between devices with their start and end apart: 0 -> 4, of which waited for: 0 -> 2; matrix products, arithmetic and copies ran while one was open for 0% -> 0% of each run, Pallas kernels for 0% -> 5%
where the time goes in v4:
time: 181 us; the launch traced here: 182 us
  blocking collectives  141 us (78%)
  Pallas kernels  29.5 us (16%)
  starting transfers between devices  5.38 us (3%)
  waiting for transfers between devices  3.29 us (2%)
    all_to_all x1, blocking collectives, packed(): incoming = lax.all_to_all(slotted, 'fsdp', 0, 0, tiled=True)  78.2 us
    all_to_all x1, blocking collectives, per_device(): received = lax.all_to_all(outgoing, ('fsdp', 'tp'), 0, 0, tiled=True)  62.7 us
    pallas_call x1, Pallas kernels, place_columns(): pl.pallas_call(functools.partial(place_kernel, capacity), grid_spec=pltpu...  9.09 us
    pallas_call x1, Pallas kernels, local_rotation(): pl.pallas_call(local_kernel, grid=(steps,), in_specs=[pl.BlockSpec((1, BL...  8.32 us
    pallas_call x1, Pallas kernels, quantize_blocks(): pl.pallas_call(quantize_kernel, in_specs=[pl.BlockSpec(memory_space=pltpu...  6.52 us
    ppermute x4, starting transfers between devices, shifted(): return lax.ppermute(value, 'fsdp', pairs)  5.38 us
    pallas_call x1, Pallas kernels, patch_hot_rank(): pl.pallas_call(patch_kernel, in_specs=[pl.BlockSpec(memory_space=pltpu.SM...  3.72 us
  transfers between devices with their start and end apart: 4, of which 2 were waited for; matrix products, arithmetic and copies ran while one was open for 0% of the time, Pallas kernels for 5%

profile of v4, /device:TPU:6, one launch (start us, length us, event | category | flops | bytes accessed | tf_op | source)
XLA Modules:
  0.0 181.8 jit_solution(188570852351149403)
XLA Ops:
  0.6 8.3 %local_rotation.1 = (bf16[2,8,8,8,16,128]{5,4,3,2,1,0:T(8,128)(2,1)}, s32[8,128]{1,0:T(8,128)S(1)}) custom-call(s32[1,128]{1,0:T(1,128)} %bitcast.7, f32[1024,2048]{1,0:T(8,128)} %w_ref.1), custom_call_target="tpu_custom_call" | custom-call | tf_op jit(solution)/shard_map/local_rotation/pallas_call | solution.py:132
  9.0 62.7 %all_to_all.15 = bf16[128,128,128]{2,1,0:T(8,128)(2,1)} all-to-all(bf16[128,128,128]{2,1,0:T(8,128)(2,1)} %bitcast.6), channel_id=1, replica_groups=mesh['fsdp'=16,'tp'=8] {'fsdp','tp'}, dimensions={0} | all-to-all | bytes 8388608 | tf_op jit(solution)/shard_map/all_to_all | solution.py:417
  71.7 0.5 slice.3
  72.8 108.9 %conditional.1 = ((bf16[2048,2048]{1,0:T(8,128)(2,1)}, bf16[16,2048]{1,0:T(8,128)(2,1)})) conditional(s32[]{:T(128)} %bitcast.3, (s32[8,128]{1,0:T(8,128)S(1)}, bf16[128,8,16,128]{3,2,1,0:T(8,128)(2,1)}) %tuple.25, (s32[8,128]{1,0:T(8,128)S(1)}, bf16[128,8,16,128]{3,2,1,0:T(8,128)(2,1)}) %tuple.26), branch_computations={%region_0.0_spmd, %region_1.0_spmd} | conditional | flops 1073741824 | bytes 46268712 | solution.py:420
  72.9 6.5 %quantize_blocks.3 = bf16[16,1552,128]{2,1,0:T(8,128)(2,1)} custom-call(s32[8,128]{1,0:T(8,128)S(1)} %get-tuple-element.10.meta_ref, bf16[128,8,16,128]{3,2,1,0:T(8,128)(2,1)} %get-tuple-element.11.in_ref), custom_call_target="tpu_custom_call" | custom-call | tf_op jit(solution)/shard_map/cond/branch_1_fun/quantize_blocks/pallas_call | solution.py:232
  79.4 78.2 %all_to_all.14.in_ref.refs_0_.refs_1_.refs_2_.refs_3_.refs_4_ = bf16[16,1552,128]{2,1,0:T(8,128)(2,1)} all-to-all(bf16[16,1552,128]{2,1,0:T(8,128)(2,1)} %quantize_blocks.3), channel_id=1, replica_groups=mesh['fsdp'=16,'tp'=8] {'fsdp'}, dimensions={0} | all-to-all | bytes 12713984 | tf_op jit(solution)/shard_map/cond/branch_1_fun/all_to_all | solution.py:407
  157.6 1.9 %last_position.1 = bf16[16,128,128]{2,1,0:T(8,128)(2,1)} custom-call(bf16[16,1552,128]{2,1,0:T(8,128)(2,1)} %all_to_all.14.in_ref.refs_0_.refs_1_.refs_2_.refs_3_.refs_4_), custom_call_target="tpu_custom_call" | custom-call | tf_op jit(solution)/shard_map/cond/branch_1_fun/last_position/pallas_call | solution.py:335
  159.5 0.6 collective-permute-start.3
  160.0 2.7 %collective-permute-start.2 = (bf16[16,128,128]{2,1,0:T(8,128)(2,1)}, bf16[16,128,128]{2,1,0:T(8,128)(2,1)S(1)}, u32[]{:S(2)}, u32[]{:S(2)}) collective-permute-start(bf16[16,128,128]{2,1,0:T(8,128)(2,1)} %last_position.1), channel_id=1, source_target_pairs={{0,24},{8,0},{16,8},{24,16},{32,56},{40,32},{48,40},{56,48},{64,88... | collective-permute-start | bytes 1572872 | tf_op jit(solution)/shard_map/cond/branch_1_fun/ppermute | solution.py:396
  162.7 2.1 %collective-permute-start.1 = (bf16[16,128,128]{2,1,0:T(8,128)(2,1)}, bf16[16,128,128]{2,1,0:T(8,128)(2,1)S(1)}, u32[]{:S(2)}, u32[]{:S(2)}) collective-permute-start(bf16[16,128,128]{2,1,0:T(8,128)(2,1)} %last_position.1), channel_id=1, source_target_pairs={{0,32},{8,40},{16,48},{24,56},{32,64},{40,72},{48,80},{56,88},{64,... | collective-permute-start | bytes 1572872 | tf_op jit(solution)/shard_map/cond/branch_1_fun/ppermute | solution.py:396
  164.8 0.0 collective-permute-start
  164.8 9.1 %place_columns.3 = (bf16[2048,2048]{1,0:T(8,128)(2,1)}, bf16[16,2048]{1,0:T(8,128)(2,1)}) custom-call(s32[8,128]{1,0:T(8,128)S(1)} %get-tuple-element.10.meta_ref, bf16[16,1552,128]{2,1,0:T(8,128)(2,1)} %all_to_all.14.in_ref.refs_0_.refs_1_.refs_2_.refs_3_.refs_4_, bf16[16,1552,128]{2,1,0:T(8,128)(2,1)} %all_to_all.14.in_ref.refs_0_.refs_1_.refs_2_.refs_3_.refs_4_, ...), custom_call_target="tpu_custom_call" | custom-call | flops 1073741824 | bytes 16777216 | tf_op jit(solution)/shard_map/cond/branch_1_fun/place_columns/pallas_call | solution.py:301
  173.9 0.0 collective-permute-done.3.near_3
  173.9 0.0 copy-start
  173.9 0.0 collective-permute-done.2.near_2
  173.9 0.0 copy-start.1
  174.0 0.4 collective-permute-done.1.near_1
  174.4 2.9 %collective-permute-done.near_0 = bf16[16,128,128]{2,1,0:T(8,128)(2,1)S(1)} collective-permute-done((bf16[16,128,128]{2,1,0:T(8,128)(2,1)}, bf16[16,128,128]{2,1,0:T(8,128)(2,1)S(1)}, u32[]{:S(2)}, u32[]{:S(2)}) %collective-permute-start) | collective-permute-done | bytes 524320 | tf_op jit(solution)/shard_map/cond/branch_1_fun/ppermute | solution.py:396
  177.2 0.0 copy-start.3
  177.3 0.0 copy-done
  177.3 0.0 copy-done.1
  177.3 0.0 copy-done.2
  177.3 0.8 copy-done.3
  178.1 3.7 %patch_hot_rank.1 = bf16[2048,2048]{1,0:T(8,128)(2,1)} custom-call(s32[8,128]{1,0:T(8,128)S(1)} %get-tuple-element.10.meta_ref, bf16[16,128,128]{2,1,0:T(8,128)(2,1)} %copy-done.3, bf16[16,128,128]{2,1,0:T(8,128)(2,1)} %copy-done.2, bf16[16,128,128]{2,1,0:T(8,128)(2,1)} %copy-done.1, bf16[16,128,128]{2,1,0:T(8,128)(2,1)} %copy-done, ...), custom_call_target="tpu_custom_call", output_to_operand_aliasing={{}: (5, {})} | custom-call | tf_op jit(solution)/shard_map/cond/branch_1_fun/patch_hot_rank/pallas_call | solution.py:373
  (1 shorter events, 0.0 us)
Async XLA Ops:
  159.5 14.5 %collective-permute-start.3 = (bf16[16,128,128]{2,1,0:T(8,128)(2,1)}, bf16[16,128,128]{2,1,0:T(8,128)(2,1)S(1)}, u32[]{:S(2)}, u32[]{:S(2)}) collective-permute-start(bf16[16,128,128]{2,1,0:T(8,128)(2,1)} %last_position.1), channel_id=1, source_target_pairs={{0,8},{8,16},{16,24},{24,0},{32,40},{40,48},{48,56},{56,32},{64,72... | collective-permute-start | bytes 1572872 | tf_op jit(solution)/shard_map/cond/branch_1_fun/ppermute | solution.py:396
  160.0 13.9 %collective-permute-start.2 = (bf16[16,128,128]{2,1,0:T(8,128)(2,1)}, bf16[16,128,128]{2,1,0:T(8,128)(2,1)S(1)}, u32[]{:S(2)}, u32[]{:S(2)}) collective-permute-start(bf16[16,128,128]{2,1,0:T(8,128)(2,1)} %last_position.1), channel_id=1, source_target_pairs={{0,24},{8,0},{16,8},{24,16},{32,56},{40,32},{48,40},{56,48},{64,88... | collective-permute-start | bytes 1572872 | tf_op jit(solution)/shard_map/cond/branch_1_fun/ppermute | solution.py:396
  162.7 11.7 %collective-permute-start.1 = (bf16[16,128,128]{2,1,0:T(8,128)(2,1)}, bf16[16,128,128]{2,1,0:T(8,128)(2,1)S(1)}, u32[]{:S(2)}, u32[]{:S(2)}) collective-permute-start(bf16[16,128,128]{2,1,0:T(8,128)(2,1)} %last_position.1), channel_id=1, source_target_pairs={{0,32},{8,40},{16,48},{24,56},{32,64},{40,72},{48,80},{56,88},{64,... | collective-permute-start | bytes 1572872 | tf_op jit(solution)/shard_map/cond/branch_1_fun/ppermute | solution.py:396
  164.8 12.4 %collective-permute-start = (bf16[16,128,128]{2,1,0:T(8,128)(2,1)}, bf16[16,128,128]{2,1,0:T(8,128)(2,1)S(1)}, u32[]{:S(2)}, u32[]{:S(2)}) collective-permute-start(bf16[16,128,128]{2,1,0:T(8,128)(2,1)} %last_position.1), channel_id=1, source_target_pairs={{0,96},{8,104},{16,112},{24,120},{32,0},{40,8},{48,16},{56,24},{64... | collective-permute-start | bytes 1572872 | tf_op jit(solution)/shard_map/cond/branch_1_fun/ppermute | solution.py:396
  173.9 3.3 %copy-start = (bf16[16,128,128]{2,1,0:T(8,128)(2,1)}, bf16[16,128,128]{2,1,0:T(8,128)(2,1)S(1)}, u32[]{:S(2)}) copy-start(bf16[16,128,128]{2,1,0:T(8,128)(2,1)S(1)} %collective-permute-done.3.near_3) | copy-start | bytes 1572868 | tf_op jit(solution)/shard_map/cond
  173.9 3.3 %copy-start.1 = (bf16[16,128,128]{2,1,0:T(8,128)(2,1)}, bf16[16,128,128]{2,1,0:T(8,128)(2,1)S(1)}, u32[]{:S(2)}) copy-start(bf16[16,128,128]{2,1,0:T(8,128)(2,1)S(1)} %collective-permute-done.2.near_2) | copy-start | bytes 1572868 | tf_op jit(solution)/shard_map/cond
  174.4 2.9 %copy-start.2 = (bf16[16,128,128]{2,1,0:T(8,128)(2,1)}, bf16[16,128,128]{2,1,0:T(8,128)(2,1)S(1)}, u32[]{:S(2)}) copy-start(bf16[16,128,128]{2,1,0:T(8,128)(2,1)S(1)} %collective-permute-done.1.near_1) | copy-start | bytes 1572868 | tf_op jit(solution)/shard_map/cond
  177.2 0.8 copy-start.3

commit v5 on v4

--- a/solution.py
+++ b/solution.py
@@ -12,7 +12,7 @@
 GROUP = 16
 EIGHT = 8
 SHARDS = 16
-TILES = 4
+TILES = 8
 PAIRS = 4
 STEP_SLOTS = 4
 SIDE = 4
@@ -322,6 +322,7 @@
             bytes_accessed=4 * SHARDS * BLOCK * cols,
             transcendentals=0,
         ),
+        compiler_params=pltpu.CompilerParams(vmem_limit_bytes=46 << 20),
         name="place_columns",
     )(meta, *[incoming] * (STEP_SLOTS + 1))
 
@@ -338,6 +339,7 @@
         in_specs=[pl.BlockSpec(shape, lambda s: (0, PACKED - 1, 0))],
         out_specs=pl.BlockSpec(shape, lambda s: (0, 0, 0)),
         out_shape=jax.ShapeDtypeStruct(shape, BF16),
+        compiler_params=pltpu.CompilerParams(vmem_limit_bytes=4 << 20),
         name="last_position",
     )(incoming)
 
@@ -384,6 +386,7 @@
             pltpu.SemaphoreType.DMA((4,)),
         ],
         input_output_aliases={5: 0},
+        compiler_params=pltpu.CompilerParams(vmem_limit_bytes=50 << 20),
         name="patch_hot_rank",
     )(meta, *nears, rolled)
 

time: 181 us -> 174 us (0.961)
  Pallas kernels: 29.5 us -> 21 us
  waiting for transfers between devices: 3.29 us -> 5.64 us
    pallas_call x1, Pallas kernels: 3.72 us -> 0.69 us  [patch_hot_rank(): pl.pallas_call(patch_kernel, in_specs=[pl.BlockSpec(memory_space=pltpu.SM...]
    pallas_call x1, Pallas kernels: 9.09 us -> 6.48 us  [place_columns(): pl.pallas_call(functools.partial(place_kernel, capacity), grid_spec=pltpu...]
    ppermute x4, waiting for transfers between devices: 3.29 us -> 5.64 us  [shifted(): return lax.ppermute(value, 'fsdp', pairs)]
    pallas_call x1, Pallas kernels: 1.88 us -> 0.07 us  [last_position(): pl.pallas_call(copy_kernel, grid=(1,), in_specs=[pl.BlockSpec(shape, lamb...]
  transfers between devices with their start and end apart: 4 -> 4, of which waited for: 2 -> 3; matrix products, arithmetic and copies ran while one was open for 0% -> 0% of each run, Pallas kernels for 5% -> 4%
where the time goes in v5:
time: 174 us
  blocking collectives  140 us (80%)
  Pallas kernels  21 us (12%)
  waiting for transfers between devices  5.64 us (3%)
  starting transfers between devices  5.42 us (3%)
    all_to_all x1, blocking collectives, packed(): incoming = lax.all_to_all(slotted, 'fsdp', 0, 0, tiled=True)  77.5 us
    all_to_all x1, blocking collectives, per_device(): received = lax.all_to_all(outgoing, ('fsdp', 'tp'), 0, 0, tiled=True)  62.7 us
    pallas_call x1, Pallas kernels, local_rotation(): pl.pallas_call(local_kernel, grid=(steps,), in_specs=[pl.BlockSpec((1, BL...  7.28 us
    pallas_call x1, Pallas kernels, quantize_blocks(): pl.pallas_call(quantize_kernel, in_specs=[pl.BlockSpec(memory_space=pltpu...  6.5 us
    pallas_call x1, Pallas kernels, place_columns(): pl.pallas_call(functools.partial(place_kernel, capacity), grid_spec=pltpu...  6.48 us
    ppermute x4, waiting for transfers between devices, shifted(): return lax.ppermute(value, 'fsdp', pairs)  5.64 us
    ppermute x4, starting transfers between devices, shifted(): return lax.ppermute(value, 'fsdp', pairs)  5.42 us
  transfers between devices with their start and end apart: 4, of which 3 were waited for; matrix products, arithmetic and copies ran while one was open for 0% of the time, Pallas kernels for 4%

profile of v5, /device:TPU:6, one launch (start us, length us, event | category | flops | bytes accessed | tf_op | source)
XLA Modules:
  0.0 174.1 jit_solution(17310974416640213141)
XLA Ops:
  0.6 7.3 %local_rotation.1 = (bf16[2,8,8,8,16,128]{5,4,3,2,1,0:T(8,128)(2,1)}, s32[8,128]{1,0:T(8,128)S(1)}) custom-call(s32[1,128]{1,0:T(1,128)} %bitcast.7, f32[1024,2048]{1,0:T(8,128)} %w_ref.1), custom_call_target="tpu_custom_call" | custom-call | tf_op jit(solution)/shard_map/local_rotation/pallas_call | solution.py:132
  7.9 62.7 %all_to_all.15 = bf16[128,128,128]{2,1,0:T(8,128)(2,1)} all-to-all(bf16[128,128,128]{2,1,0:T(8,128)(2,1)} %bitcast.6), channel_id=1, replica_groups=mesh['fsdp'=16,'tp'=8] {'fsdp','tp'}, dimensions={0} | all-to-all | bytes 8388608 | tf_op jit(solution)/shard_map/all_to_all | solution.py:420
  70.6 0.5 slice.3
  71.8 102.3 %conditional.1 = ((bf16[2048,2048]{1,0:T(8,128)(2,1)}, bf16[16,2048]{1,0:T(8,128)(2,1)})) conditional(s32[]{:T(128)} %bitcast.3, (s32[8,128]{1,0:T(8,128)S(1)}, bf16[128,8,16,128]{3,2,1,0:T(8,128)(2,1)}) %tuple.25, (s32[8,128]{1,0:T(8,128)S(1)}, bf16[128,8,16,128]{3,2,1,0:T(8,128)(2,1)}) %tuple.26), branch_computations={%region_0.0_spmd, %region_1.0_spmd} | conditional | flops 1073741824 | bytes 37879992 | solution.py:423
  71.8 6.5 %quantize_blocks.3 = bf16[16,1552,128]{2,1,0:T(8,128)(2,1)} custom-call(s32[8,128]{1,0:T(8,128)S(1)} %get-tuple-element.10.meta_ref, bf16[128,8,16,128]{3,2,1,0:T(8,128)(2,1)} %get-tuple-element.11.in_ref), custom_call_target="tpu_custom_call" | custom-call | tf_op jit(solution)/shard_map/cond/branch_1_fun/quantize_blocks/pallas_call | solution.py:232
  78.3 77.5 %all_to_all.14.in_ref.refs_0_.refs_1_.refs_2_.refs_3_.refs_4_ = bf16[16,1552,128]{2,1,0:T(8,128)(2,1)S(1)} all-to-all(bf16[16,1552,128]{2,1,0:T(8,128)(2,1)} %quantize_blocks.3), channel_id=1, replica_groups=mesh['fsdp'=16,'tp'=8] {'fsdp'}, dimensions={0} | all-to-all | bytes 12713984 | tf_op jit(solution)/shard_map/cond/branch_1_fun/all_to_all | solution.py:410
  155.8 0.1 last_position.1
  155.9 0.6 collective-permute-start.3
  156.5 2.7 %collective-permute-start.2 = (bf16[16,128,128]{2,1,0:T(8,128)(2,1)S(1)}, bf16[16,128,128]{2,1,0:T(8,128)(2,1)S(1)}, u32[]{:S(2)}, u32[]{:S(2)}) collective-permute-start(bf16[16,128,128]{2,1,0:T(8,128)(2,1)S(1)} %last_position.1), channel_id=1, source_target_pairs={{0,24},{8,0},{16,8},{24,16},{32,56},{40,32},{48,40},{56,48},{64,88... | collective-permute-start | bytes 1572872 | tf_op jit(solution)/shard_map/cond/branch_1_fun/ppermute | solution.py:399
  159.2 2.1 %collective-permute-start.1 = (bf16[16,128,128]{2,1,0:T(8,128)(2,1)S(1)}, bf16[16,128,128]{2,1,0:T(8,128)(2,1)S(1)}, u32[]{:S(2)}, u32[]{:S(2)}) collective-permute-start(bf16[16,128,128]{2,1,0:T(8,128)(2,1)S(1)} %last_position.1), channel_id=1, source_target_pairs={{0,32},{8,40},{16,48},{24,56},{32,64},{40,72},{48,80},{56,88},{64,... | collective-permute-start | bytes 1572872 | tf_op jit(solution)/shard_map/cond/branch_1_fun/ppermute | solution.py:399
  161.3 0.0 collective-permute-start
  161.3 6.5 %place_columns.3 = (bf16[2048,2048]{1,0:T(8,128)(2,1)}, bf16[16,2048]{1,0:T(8,128)(2,1)}) custom-call(s32[8,128]{1,0:T(8,128)S(1)} %get-tuple-element.10.meta_ref, bf16[16,1552,128]{2,1,0:T(8,128)(2,1)S(1)} %all_to_all.14.in_ref.refs_0_.refs_1_.refs_2_.refs_3_.refs_4_, bf16[16,1552,128]{2,1,0:T(8,128)(2,1)S(1)} %all_to_all.14.in_ref.refs_0_.refs_1_.refs_2_.refs_3_.refs_4_, ...), custom_call_target="tpu_custom_call" | custom-call | flops 1073741824 | bytes 16777216 | tf_op jit(solution)/shard_map/cond/branch_1_fun/place_columns/pallas_call | solution.py:301
  167.8 1.2 collective-permute-done.3.near_3
  169.0 0.0 collective-permute-done.2.near_2
  169.0 1.5 collective-permute-done.1.near_1
  170.4 3.0 %collective-permute-done.near_0 = bf16[16,128,128]{2,1,0:T(8,128)(2,1)S(1)} collective-permute-done((bf16[16,128,128]{2,1,0:T(8,128)(2,1)S(1)}, bf16[16,128,128]{2,1,0:T(8,128)(2,1)S(1)}, u32[]{:S(2)}, u32[]{:S(2)}) %collective-permute-start) | collective-permute-done | bytes 524320 | tf_op jit(solution)/shard_map/cond/branch_1_fun/ppermute | solution.py:399
  173.4 0.7 patch_hot_rank.1
Async XLA Ops:
  155.9 13.1 %collective-permute-start.3 = (bf16[16,128,128]{2,1,0:T(8,128)(2,1)S(1)}, bf16[16,128,128]{2,1,0:T(8,128)(2,1)S(1)}, u32[]{:S(2)}, u32[]{:S(2)}) collective-permute-start(bf16[16,128,128]{2,1,0:T(8,128)(2,1)S(1)} %last_position.1), channel_id=1, source_target_pairs={{0,8},{8,16},{16,24},{24,0},{32,40},{40,48},{48,56},{56,32},{64,72... | collective-permute-start | bytes 1572872 | tf_op jit(solution)/shard_map/cond/branch_1_fun/ppermute | solution.py:399
  156.5 12.4 %collective-permute-start.2 = (bf16[16,128,128]{2,1,0:T(8,128)(2,1)S(1)}, bf16[16,128,128]{2,1,0:T(8,128)(2,1)S(1)}, u32[]{:S(2)}, u32[]{:S(2)}) collective-permute-start(bf16[16,128,128]{2,1,0:T(8,128)(2,1)S(1)} %last_position.1), channel_id=1, source_target_pairs={{0,24},{8,0},{16,8},{24,16},{32,56},{40,32},{48,40},{56,48},{64,88... | collective-permute-start | bytes 1572872 | tf_op jit(solution)/shard_map/cond/branch_1_fun/ppermute | solution.py:399
  159.2 11.2 %collective-permute-start.1 = (bf16[16,128,128]{2,1,0:T(8,128)(2,1)S(1)}, bf16[16,128,128]{2,1,0:T(8,128)(2,1)S(1)}, u32[]{:S(2)}, u32[]{:S(2)}) collective-permute-start(bf16[16,128,128]{2,1,0:T(8,128)(2,1)S(1)} %last_position.1), channel_id=1, source_target_pairs={{0,32},{8,40},{16,48},{24,56},{32,64},{40,72},{48,80},{56,88},{64,... | collective-permute-start | bytes 1572872 | tf_op jit(solution)/shard_map/cond/branch_1_fun/ppermute | solution.py:399
  161.3 12.1 %collective-permute-start = (bf16[16,128,128]{2,1,0:T(8,128)(2,1)S(1)}, bf16[16,128,128]{2,1,0:T(8,128)(2,1)S(1)}, u32[]{:S(2)}, u32[]{:S(2)}) collective-permute-start(bf16[16,128,128]{2,1,0:T(8,128)(2,1)S(1)} %last_position.1), channel_id=1, source_target_pairs={{0,96},{8,104},{16,112},{24,120},{32,0},{40,8},{48,16},{56,24},{64... | collective-permute-start | bytes 1572872 | tf_op jit(solution)/shard_map/cond/branch_1_fun/ppermute | solution.py:399

commit v6 on v5

--- a/solution.py
+++ b/solution.py
@@ -16,8 +16,8 @@
 PAIRS = 4
 STEP_SLOTS = 4
 SIDE = 4
-PACKED = 12
-META_RANK, META_POS, META_SLOT, META_HOT, META_FITS, META_OWNER = range(6)
+CAPACITIES = (16, 13, 12)
+META_RANK, META_POS, META_SLOT, META_HOT, META_LEVEL, META_OWNER = range(6)
 F32 = jnp.float32
 BF16 = jnp.bfloat16
 
@@ -78,16 +78,26 @@
         (x << 2) | ((z - 1) & (SIDE - 1)),
     ]
     is_hot = owner_row == hot
-    is_near = functools.reduce(jnp.logical_or, [owner_row == near for near in around])
-    load = jnp.where(is_hot, 0, total + is_near.astype(jnp.int32))
-    fits = (jnp.max(load, axis=1, keepdims=True) <= PACKED) & (hot >= 0)
-    fits = jnp.broadcast_to(fits.astype(jnp.int32), owner_row.shape) != 0
-    over = is_hot & (position >= PACKED) & fits
+    level = jnp.zeros_like(hot)
+    capacity = jnp.full_like(hot, SHARDS)
+    for choice in (1, 2):
+        size = CAPACITIES[choice]
+        is_near = functools.reduce(
+            jnp.logical_or, [owner_row == near for near in around[: SHARDS - size]]
+        )
+        load = jnp.where(is_hot, 0, total + is_near.astype(jnp.int32))
+        good = (jnp.max(load, axis=1, keepdims=True) <= size) & (hot >= 0)
+        level = jnp.where(good, choice, level)
+        capacity = jnp.where(good, size, capacity)
+    level = jnp.broadcast_to(level, owner_row.shape)
+    capacity = jnp.broadcast_to(capacity, owner_row.shape)
+    fits = level > 0
+    over = is_hot & (position >= capacity) & fits
     rank = owner_row
     for d, near in enumerate(around):
-        rank = jnp.where(over & (position == PACKED + d), near, rank)
+        rank = jnp.where(over & (position == capacity + d), near, rank)
     block = lane[:1]
-    position = jnp.where(fits, jnp.where(over, PACKED - 1, position), block >> 3)
+    position = jnp.where(fits, jnp.where(over, capacity - 1, position), block >> 3)
     mine = (by_row == me.astype(F32)) & ((row >> 3) == lane)
     slot = jnp.sum(
         jnp.where(mine, (position_by_row + 1).astype(F32), 0.0), axis=0, keepdims=True
@@ -97,7 +107,7 @@
     meta_ref[META_POS : META_POS + 1, :] = position
     meta_ref[META_SLOT : META_SLOT + 1, :] = slot
     meta_ref[META_HOT : META_HOT + 1, :] = jnp.broadcast_to(hot, owner_row.shape)
-    meta_ref[META_FITS : META_FITS + 1, :] = fits.astype(jnp.int32)
+    meta_ref[META_LEVEL : META_LEVEL + 1, :] = level
     meta_ref[META_OWNER : META_OWNER + 1, :] = owner_row
 
 
@@ -331,12 +341,12 @@
     out_ref[...] = in_ref[...]
 
 
-def last_position(incoming):
+def last_position(incoming, capacity):
     shape = (SHARDS, BLOCK, LANES)
     return pl.pallas_call(
         copy_kernel,
         grid=(1,),
-        in_specs=[pl.BlockSpec(shape, lambda s: (0, PACKED - 1, 0))],
+        in_specs=[pl.BlockSpec(shape, lambda s: (0, capacity - 1, 0))],
         out_specs=pl.BlockSpec(shape, lambda s: (0, 0, 0)),
         out_shape=jax.ShapeDtypeStruct(shape, BF16),
         compiler_params=pltpu.CompilerParams(vmem_limit_bytes=4 << 20),
@@ -344,14 +354,15 @@
     )(incoming)
 
 
-def patch_kernel(
-    meta_ref, near_0, near_1, near_2, near_3, _, out_ref, nears, buffers, eye_ref, in_sem, sem
-):
+def patch_kernel(capacity, meta_ref, *refs):
+    count = SHARDS - capacity
+    arrived, (_, out_ref, nears, buffers, eye_ref, in_sem, sem) = refs[:count], refs[count:]
+
     @pl.when(meta_ref[META_HOT, 0] == lax.axis_index("fsdp"))
     def _():
         loads = [
             pltpu.make_async_copy(near, nears.at[d], in_sem.at[d])
-            for d, near in enumerate((near_0, near_1, near_2, near_3))
+            for d, near in enumerate(arrived)
         ]
         for load in loads:
             load.start()
@@ -362,7 +373,7 @@
             place_block(eye_ref[...], nears.at[d], buffers.at[d])
             stores.append(
                 pltpu.make_async_copy(
-                    buffers.at[d], out_ref.at[pl.ds((PACKED + d) * BLOCK, BLOCK), :], sem.at[d]
+                    buffers.at[d], out_ref.at[pl.ds((capacity + d) * BLOCK, BLOCK), :], sem.at[d]
                 )
             )
             stores[-1].start()
@@ -372,20 +383,21 @@
 
 def patch_hot_rank(meta, rolled, nears):
     cols = rolled.shape[1]
+    count = len(nears)
     return pl.pallas_call(
-        patch_kernel,
+        functools.partial(patch_kernel, SHARDS - count),
         in_specs=[pl.BlockSpec(memory_space=pltpu.SMEM)]
-        + [pl.BlockSpec(memory_space=pl.ANY)] * 5,
+        + [pl.BlockSpec(memory_space=pl.ANY)] * (count + 1),
         out_specs=pl.BlockSpec(memory_space=pl.ANY),
         out_shape=jax.ShapeDtypeStruct(rolled.shape, rolled.dtype),
         scratch_shapes=[
-            pltpu.VMEM((4, SHARDS, BLOCK, LANES), BF16),
-            pltpu.VMEM((4, BLOCK, cols), BF16),
+            pltpu.VMEM((count, SHARDS, BLOCK, LANES), BF16),
+            pltpu.VMEM((count, BLOCK, cols), BF16),
             pltpu.VMEM((BLOCK, BLOCK), BF16),
-            pltpu.SemaphoreType.DMA((4,)),
-            pltpu.SemaphoreType.DMA((4,)),
-        ],
-        input_output_aliases={5: 0},
+            pltpu.SemaphoreType.DMA((count,)),
+            pltpu.SemaphoreType.DMA((count,)),
+        ],
+        input_output_aliases={count + 1: 0},
         compiler_params=pltpu.CompilerParams(vmem_limit_bytes=50 << 20),
         name="patch_hot_rank",
     )(meta, *nears, rolled)
@@ -405,12 +417,13 @@
     return tuple(place_columns(meta, incoming, SHARDS))
 
 
-def packed(meta, received):
-    slotted = quantize_blocks(meta, received, PACKED)
+def packed(capacity, meta, received):
+    slotted = quantize_blocks(meta, received, capacity)
     incoming = lax.all_to_all(slotted, "fsdp", 0, 0, tiled=True)
-    foreign = last_position(incoming)
-    nears = [shifted(foreign, dx, dz) for dx, dz in ((-1, 0), (1, 0), (0, -1), (0, 1))]
-    rolled, rolled_scales = place_columns(meta, incoming, PACKED)
+    foreign = last_position(incoming, capacity)
+    ways = ((-1, 0), (1, 0), (0, -1), (0, 1))[: SHARDS - capacity]
+    nears = [shifted(foreign, dx, dz) for dx, dz in ways]
+    rolled, rolled_scales = place_columns(meta, incoming, capacity)
     return patch_hot_rank(meta, rolled, nears), rolled_scales
 
 
@@ -420,7 +433,12 @@
     received = lax.all_to_all(outgoing, ("fsdp", "tp"), 0, 0, tiled=True)
     received = received.reshape(SHARDS * EIGHT, EIGHT, GROUP, BLOCK)
     received, meta = lax.optimization_barrier((received, meta))
-    return lax.cond(meta[META_FITS, 0] != 0, packed, general, meta, received)
+    return lax.switch(
+        meta[META_LEVEL, 0],
+        [general] + [functools.partial(packed, size) for size in CAPACITIES[1:]],
+        meta,
+        received,
+    )
 
 
 def solution(mesh):

time: 174 us -> 176 us (1.011); the launches traced: 174 us -> 174 us
  no operation moved by 1% of the time
where the time goes in v6:
time: 176 us; the launch traced here: 174 us
  blocking collectives  140 us (80%)
  Pallas kernels  21.5 us (12%)
  starting transfers between devices  5.42 us (3%)
  waiting for transfers between devices  5.17 us (3%)
    all_to_all x1, blocking collectives, packed(): incoming = lax.all_to_all(slotted, 'fsdp', 0, 0, tiled=True)  77.4 us
    all_to_all x1, blocking collectives, per_device(): received = lax.all_to_all(outgoing, ('fsdp', 'tp'), 0, 0, tiled=True)  62.7 us
    pallas_call x1, Pallas kernels, local_rotation(): pl.pallas_call(local_kernel, grid=(steps,), in_specs=[pl.BlockSpec((1, BL...  7.28 us
    pallas_call x1, Pallas kernels, place_columns(): pl.pallas_call(functools.partial(place_kernel, capacity), grid_spec=pltpu...  6.96 us
    pallas_call x1, Pallas kernels, quantize_blocks(): pl.pallas_call(quantize_kernel, in_specs=[pl.BlockSpec(memory_space=pltpu...  6.54 us
    ppermute x4, starting transfers between devices, shifted(): return lax.ppermute(value, 'fsdp', pairs)  5.42 us
    ppermute x4, waiting for transfers between devices, shifted(): return lax.ppermute(value, 'fsdp', pairs)  5.17 us
  transfers between devices with their start and end apart: 4, of which 3 were waited for; matrix products, arithmetic and copies ran while one was open for 0% of the time, Pallas kernels for 4%

profile of v6, /device:TPU:6, one launch (start us, length us, event | category | flops | bytes accessed | tf_op | source)
XLA Modules:
  0.0 174.1 jit_solution(13976331090164308642)
XLA Ops:
  0.6 7.3 %local_rotation.1 = (bf16[2,8,8,8,16,128]{5,4,3,2,1,0:T(8,128)(2,1)}, s32[8,128]{1,0:T(8,128)S(1)}) custom-call(s32[1,128]{1,0:T(1,128)} %bitcast.8, f32[1024,2048]{1,0:T(8,128)} %w_ref.1), custom_call_target="tpu_custom_call" | custom-call | tf_op jit(solution)/shard_map/local_rotation/pallas_call | solution.py:142
  7.9 62.7 %all_to_all.20 = bf16[128,128,128]{2,1,0:T(8,128)(2,1)} all-to-all(bf16[128,128,128]{2,1,0:T(8,128)(2,1)} %bitcast.7), channel_id=1, replica_groups=mesh['fsdp'=16,'tp'=8] {'fsdp','tp'}, dimensions={0} | all-to-all | bytes 8388608 | tf_op jit(solution)/shard_map/all_to_all | solution.py:433
  70.6 0.5 slice.3
  71.8 102.3 %conditional.1 = ((bf16[2048,2048]{1,0:T(8,128)(2,1)}, bf16[16,2048]{1,0:T(8,128)(2,1)})) conditional(s32[]{:T(128)} %bitcast.3, (s32[8,128]{1,0:T(8,128)S(1)}, bf16[128,8,16,128]{3,2,1,0:T(8,128)(2,1)}) %tuple.33, (s32[8,128]{1,0:T(8,128)S(1)}, bf16[128,8,16,128]{3,2,1,0:T(8,128)(2,1)}) %tuple.34, (s32[8,128]{1,0:T(8,128)S(1)}, ...), branch_computations={%region_0.0_spmd, %region_1.0_spmd, %region_2.0_spmd} | conditional | flops 1073741824 | bytes 37879992 | solution.py:436
  71.8 6.5 %quantize_blocks.5 = bf16[16,1552,128]{2,1,0:T(8,128)(2,1)} custom-call(s32[8,128]{1,0:T(8,128)S(1)} %get-tuple-element.18.meta_ref, bf16[128,8,16,128]{3,2,1,0:T(8,128)(2,1)} %get-tuple-element.19.in_ref), custom_call_target="tpu_custom_call" | custom-call | tf_op jit(solution)/shard_map/cond/branch_2_fun/quantize_blocks/pallas_call | solution.py:242
  78.4 77.4 %all_to_all.19.in_ref.refs_0_.refs_1_.refs_2_.refs_3_.refs_4_ = bf16[16,1552,128]{2,1,0:T(8,128)(2,1)S(1)} all-to-all(bf16[16,1552,128]{2,1,0:T(8,128)(2,1)} %quantize_blocks.5), channel_id=1, replica_groups=mesh['fsdp'=16,'tp'=8] {'fsdp'}, dimensions={0} | all-to-all | bytes 12713984 | tf_op jit(solution)/shard_map/cond/branch_2_fun/all_to_all | solution.py:422
  155.8 0.1 last_position.3
  155.9 0.6 collective-permute-start.6
  156.5 2.7 %collective-permute-start.5 = (bf16[16,128,128]{2,1,0:T(8,128)(2,1)S(1)}, bf16[16,128,128]{2,1,0:T(8,128)(2,1)S(1)}, u32[]{:S(2)}, u32[]{:S(2)}) collective-permute-start(bf16[16,128,128]{2,1,0:T(8,128)(2,1)S(1)} %last_position.3), channel_id=1, source_target_pairs={{0,24},{8,0},{16,8},{24,16},{32,56},{40,32},{48,40},{56,48},{64,88... | collective-permute-start | bytes 1572872 | tf_op jit(solution)/shard_map/cond/branch_2_fun/ppermute | solution.py:411
  159.2 2.1 %collective-permute-start.4 = (bf16[16,128,128]{2,1,0:T(8,128)(2,1)S(1)}, bf16[16,128,128]{2,1,0:T(8,128)(2,1)S(1)}, u32[]{:S(2)}, u32[]{:S(2)}) collective-permute-start(bf16[16,128,128]{2,1,0:T(8,128)(2,1)S(1)} %last_position.3), channel_id=1, source_target_pairs={{0,32},{8,40},{16,48},{24,56},{32,64},{40,72},{48,80},{56,88},{64,... | collective-permute-start | bytes 1572872 | tf_op jit(solution)/shard_map/cond/branch_2_fun/ppermute | solution.py:411
  161.3 0.0 collective-permute-start.3
  161.3 7.0 %place_columns.5 = (bf16[2048,2048]{1,0:T(8,128)(2,1)}, bf16[16,2048]{1,0:T(8,128)(2,1)}) custom-call(s32[8,128]{1,0:T(8,128)S(1)} %get-tuple-element.18.meta_ref, bf16[16,1552,128]{2,1,0:T(8,128)(2,1)S(1)} %all_to_all.19.in_ref.refs_0_.refs_1_.refs_2_.refs_3_.refs_4_, bf16[16,1552,128]{2,1,0:T(8,128)(2,1)S(1)} %all_to_all.19.in_ref.refs_0_.refs_1_.refs_2_.refs_3_.refs_4_, ...), custom_call_target="tpu_custom_call" | custom-call | flops 1073741824 | bytes 16777216 | tf_op jit(solution)/shard_map/cond/branch_2_fun/place_columns/pallas_call | solution.py:311
  168.3 0.7 collective-permute-done.6.refs_3_
  169.0 0.0 collective-permute-done.5.refs_2_
  169.0 1.5 collective-permute-done.4.refs_1_
  170.4 3.0 %collective-permute-done.3.refs_0_ = bf16[16,128,128]{2,1,0:T(8,128)(2,1)S(1)} collective-permute-done((bf16[16,128,128]{2,1,0:T(8,128)(2,1)S(1)}, bf16[16,128,128]{2,1,0:T(8,128)(2,1)S(1)}, u32[]{:S(2)}, u32[]{:S(2)}) %collective-permute-start.3) | collective-permute-done | bytes 524320 | tf_op jit(solution)/shard_map/cond/branch_2_fun/ppermute | solution.py:411
  173.4 0.7 patch_hot_rank.3
Async XLA Ops:
  155.9 13.1 %collective-permute-start.6 = (bf16[16,128,128]{2,1,0:T(8,128)(2,1)S(1)}, bf16[16,128,128]{2,1,0:T(8,128)(2,1)S(1)}, u32[]{:S(2)}, u32[]{:S(2)}) collective-permute-start(bf16[16,128,128]{2,1,0:T(8,128)(2,1)S(1)} %last_position.3), channel_id=1, source_target_pairs={{0,8},{8,16},{16,24},{24,0},{32,40},{40,48},{48,56},{56,32},{64,72... | collective-permute-start | bytes 1572872 | tf_op jit(solution)/shard_map/cond/branch_2_fun/ppermute | solution.py:411
  156.5 12.4 %collective-permute-start.5 = (bf16[16,128,128]{2,1,0:T(8,128)(2,1)S(1)}, bf16[16,128,128]{2,1,0:T(8,128)(2,1)S(1)}, u32[]{:S(2)}, u32[]{:S(2)}) collective-permute-start(bf16[16,128,128]{2,1,0:T(8,128)(2,1)S(1)} %last_position.3), channel_id=1, source_target_pairs={{0,24},{8,0},{16,8},{24,16},{32,56},{40,32},{48,40},{56,48},{64,88... | collective-permute-start | bytes 1572872 | tf_op jit(solution)/shard_map/cond/branch_2_fun/ppermute | solution.py:411
  159.2 11.2 %collective-permute-start.4 = (bf16[16,128,128]{2,1,0:T(8,128)(2,1)S(1)}, bf16[16,128,128]{2,1,0:T(8,128)(2,1)S(1)}, u32[]{:S(2)}, u32[]{:S(2)}) collective-permute-start(bf16[16,128,128]{2,1,0:T(8,128)(2,1)S(1)} %last_position.3), channel_id=1, source_target_pairs={{0,32},{8,40},{16,48},{24,56},{32,64},{40,72},{48,80},{56,88},{64,... | collective-permute-start | bytes 1572872 | tf_op jit(solution)/shard_map/cond/branch_2_fun/ppermute | solution.py:411
  161.3 12.1 %collective-permute-start.3 = (bf16[16,128,128]{2,1,0:T(8,128)(2,1)S(1)}, bf16[16,128,128]{2,1,0:T(8,128)(2,1)S(1)}, u32[]{:S(2)}, u32[]{:S(2)}) collective-permute-start(bf16[16,128,128]{2,1,0:T(8,128)(2,1)S(1)} %last_position.3), channel_id=1, source_target_pairs={{0,96},{8,104},{16,112},{24,120},{32,0},{40,8},{48,16},{56,24},{64... | collective-permute-start | bytes 1572872 | tf_op jit(solution)/shard_map/cond/branch_2_fun/ppermute | solution.py:411
